TPU v7x, 32 devices: a whole 2x2x4 slice. The times are simulated.
32 devices in a mesh: dp: 16 (over z, y, core), tensor: 2 (over x).
Axes of the slice: x: 2, y: 2, z: 4, core: 2. Of those that a mesh axis runs over, the one named last changes fastest.
Arguments:
- tokens_in: bfloat16 [2, 4096, 768], P(None, ('dp', 'tensor')), may hold values from -6 to 6
- positions: int32 [3, 2, 4096], P(None, None, ('dp', 'tensor')), may hold values from 0 to 15
- segment_ids: int32 [2, 16, 256], P(None, 'dp'), may hold values from 0 to 2, never falling along the last dimension, each value on 1 to 128 neighbouring positions
- owners: int32 [10368, 1], replicated, may hold values from 0 to 15; in each aligned block of 10368 rows (0 to 10367, 10368 to 20735, ...) at most 1296 rows name the same one
- master: float32 [20736, 1024], P('dp', 'tensor'), may hold values from -0.21875 to 0.21875
- first_moment: float32 [20736, 1024], P('dp', 'tensor'), may hold values from -112 to 112
- second_moment: float32 [20736, 1024], P('dp', 'tensor'), may hold values from 81.92 to 1638.4
- norm_gains: float32 [2, 1280], replicated, may hold values from 0.5 to 1.5
- norm_biases: float32 [2, 1280], replicated, may hold values from -4 to 4
- norm_first: float32 [4, 1280], replicated, may hold values from -256 to 256
- norm_second: float32 [4, 1280], replicated, may hold values from 2048 to 8192
- cotangent: float32 [2, 4096, 512], P(None, ('dp', 'tensor')), may hold values from -6 to 6
Outputs:
- decoded: float32 [2, 4096, 512], P(None, ('dp', 'tensor'))
- tokens_grad: float32 [2, 4096, 768], P(None, ('dp', 'tensor'))
- new_master: float32 [20736, 1024], P('dp', 'tensor')
- new_first: float32 [20736, 1024], P('dp', 'tensor')
- new_second: float32 [20736, 1024], P('dp', 'tensor')
- new_norms: float32 [4, 1280], replicated
- new_norm_first: float32 [4, 1280], replicated
- new_norm_second: float32 [4, 1280], replicated
Inputs may be any that keep to these rules, and one draw needn't show every extreme that they name: `owners`: every dp index owns at most 1296 blocks, and some index owns exactly 1296. `segment_ids`: along each sequence the tile ids never fall; each tile has 1 to 128 tokens, and some tile has exactly 128.
All inputs are finite; a program needn't handle non-finite values.
Results may differ from a plain program's by a relative error of at most 0.024.
Values may be sent and summed in bfloat16 or wider, within the bound.
A program may use at most 192 MiB of HBM per device.

v0:
```python
from functools import partial

import jax
import jax.numpy as jnp
from jax import lax
from jax.sharding import PartitionSpec as P

DE = 768
HE = 12
HDE = 64
FFE = 3072
DD = 512
HD = 16
HDD = 32
FFD = 2048
STEP = 10


NORM_EPS = 1e-06
BETA_ONE = 0.5
BETA_TWO = 0.5
LEARN_RATE = 0.03
NORM_RATE = 0.3
WEIGHT_DECAY = 0.05
ADAM_EPS = 1e-08
MASK_FILL = -1000000000.0


def sincos_part(coordinate, part_width):
    halfway = part_width // 2
    frequency = 1.0 / 10000.0 ** (jnp.arange(halfway, dtype=jnp.float32) / halfway)
    angles = coordinate.astype(jnp.float32)[:, None] * frequency[None, :]
    return jnp.concatenate([jnp.sin(angles), jnp.cos(angles)], axis=1)


def sincos_embed(positions, model_width):
    side_width = model_width // 16 * 6
    first_width = model_width - 2 * side_width
    return jnp.concatenate(
        [
            sincos_part(positions[0], first_width),
            sincos_part(positions[1], side_width),
            sincos_part(positions[2], side_width),
        ],
        axis=1,
    )


def slot_table(owners, devices, capacity):
    owner_ids = owners[:, 0]
    onehot = (owner_ids[:, None] == jnp.arange(devices, dtype=jnp.int32)[None, :]).astype(jnp.int32)
    before = jnp.cumsum(onehot, axis=0) - onehot
    owner_rank = jnp.sum(before * onehot, axis=1)
    return owner_ids * capacity + owner_rank


def weight_shapes(tensor_count):
    enc_heads = HE // tensor_count
    dec_heads = HD // tensor_count
    return [
        (DE, 3 * enc_heads * HDE),
        (enc_heads * HDE, DE),
        (DE, FFE // tensor_count),
        (FFE // tensor_count, DE),
        (DE, DD // tensor_count),
        (DD, 3 * dec_heads * HDD),
        (dec_heads * HDD, DD),
        (DD, FFD // tensor_count),
        (FFD // tensor_count, DD),
    ]


def split_flat(flat_vector, shapes):
    pieces = []
    offset = 0
    for matrix_shape in shapes:
        length = matrix_shape[0] * matrix_shape[1]
        pieces.append(flat_vector[offset : offset + length].reshape(matrix_shape))
        offset += length
    return pieces


def adamw(weights, gradient, moment_one, moment_two, decay_rate, step_rate):
    one_new = BETA_ONE * moment_one + (1.0 - BETA_ONE) * gradient
    two_new = BETA_TWO * moment_two + (1.0 - BETA_TWO) * gradient * gradient
    one_hat = one_new / (1.0 - BETA_ONE**STEP)
    two_hat = two_new / (1.0 - BETA_TWO**STEP)
    weights_new = weights - step_rate * (
        one_hat / (jnp.sqrt(two_hat) + ADAM_EPS) + decay_rate * weights
    )
    return (weights_new, one_new, two_new)


def norm_forward(values, gain_row, bias_row):
    center = values - jnp.mean(values, axis=-1, keepdims=True)
    spread = jnp.mean(center * center, axis=-1, keepdims=True)
    inverse = lax.rsqrt(spread + NORM_EPS)
    normed = center * inverse
    return (normed * gain_row + bias_row, (normed, inverse))


def norm_backward(upstream, stored, gain_row):
    normed, inverse = stored
    scaled = upstream * gain_row
    mean_one = jnp.mean(scaled, axis=-1, keepdims=True)
    mean_two = jnp.mean(scaled * normed, axis=-1, keepdims=True)
    return (
        inverse * (scaled - mean_one - normed * mean_two),
        jnp.sum(upstream * normed, axis=0),
        jnp.sum(upstream, axis=0),
    )


def inner_rows(left_side, right_side):
    return lax.dot_general(
        left_side, right_side, (((0,), (0,)), ((), ())), preferred_element_type=jnp.float32
    )


def times_transpose(left_side, right_side):
    return lax.dot_general(
        left_side, right_side, (((1,), (1,)), ((), ())), preferred_element_type=jnp.float32
    )


def gather_rows(values):
    return lax.all_gather(values, "tensor", axis=0, tiled=True)


def gather_grads(values):
    return lax.all_gather(values, "tensor", axis=0, tiled=True)


def branch_rows(values, weight):
    return lax.psum_scatter(
        jnp.dot(values, weight, preferred_element_type=jnp.float32).astype(jnp.bfloat16),
        "tensor",
        scatter_dimension=0,
        tiled=True,
    ).astype(jnp.float32)


def input_rows(values, weight):
    return lax.psum_scatter(
        times_transpose(values, weight).astype(jnp.bfloat16),
        "tensor",
        scatter_dimension=0,
        tiled=True,
    ).astype(jnp.float32)


def block_scores(queries, key_rows, mask_bias, block_start, block_rows, head_size):
    scores = jnp.einsum(
        "qhd,khd->hqk", queries, key_rows, preferred_element_type=jnp.float32
    ) * head_size ** (-0.5)
    return scores + mask_bias[None, block_start : block_start + block_rows]


def attention_forward(gathered, w_qkv, head_count, head_size, mask_bias):
    length = gathered.shape[0]
    projected = jnp.dot(gathered, w_qkv, preferred_element_type=jnp.float32).astype(jnp.bfloat16)
    projected = projected.reshape(length, 3, head_count, head_size)
    queries = projected[:, 0]
    key_rows = projected[:, 1]
    value_rows = projected[:, 2]
    block_rows = min(512, length)
    scores = block_scores(queries, key_rows, mask_bias, 0, block_rows, head_size)
    row_peak = jnp.max(scores, axis=-1, keepdims=True)
    row_total = row_peak + jnp.log(jnp.sum(jnp.exp(scores - row_peak), axis=-1, keepdims=True))
    weights = jnp.exp(scores - row_total).astype(jnp.bfloat16)
    outputs = jnp.einsum("hqk,khd->qhd", weights, value_rows, preferred_element_type=jnp.float32)
    totals = [row_total]
    attended = outputs.astype(jnp.bfloat16).reshape(length, head_count * head_size)
    return (attended, (queries, key_rows, value_rows, totals))


def attention_backward(upstream, w_out, attended, stored, head_count, head_size, mask_bias):
    queries, key_rows, value_rows, totals = stored
    length = upstream.shape[0]
    score_scale = head_size ** (-0.5)
    grad_out = inner_rows(attended, upstream)
    attended_grad = (
        times_transpose(upstream, w_out).astype(jnp.bfloat16).reshape(length, head_count, head_size)
    )
    block_rows = min(512, length)
    key_grads = jnp.zeros((length, head_count, head_size), jnp.float32)
    value_grads = jnp.zeros((length, head_count, head_size), jnp.float32)
    query_grads = []
    for number, block_start in enumerate(range(0, length, block_rows)):
        scores = block_scores(queries, key_rows, mask_bias, block_start, block_rows, head_size)
        weights = jnp.exp(scores - totals[number])
        value_grads = jnp.einsum(
            "hqk,qhd->khd",
            weights.astype(jnp.bfloat16),
            attended_grad,
            preferred_element_type=jnp.float32,
        )
        weight_grads = jnp.einsum(
            "qhd,khd->hqk", attended_grad, value_rows, preferred_element_type=jnp.float32
        )
        score_grads = (
            weights * (weight_grads - jnp.sum(weights * weight_grads, axis=-1, keepdims=True))
        ).astype(jnp.bfloat16)
        query_grads.append(
            jnp.einsum("hqk,khd->qhd", score_grads, key_rows, preferred_element_type=jnp.float32)
            * score_scale
        )
        key_grads = (
            jnp.einsum("hqk,qhd->khd", score_grads, queries, preferred_element_type=jnp.float32)
            * score_scale
        )
    projected_grad = jnp.stack([query_grads[0], key_grads, value_grads], axis=1)
    return (
        projected_grad.astype(jnp.bfloat16).reshape(length, 3 * head_count * head_size),
        grad_out,
    )


def block_forward(residual, matrices, gain_rows, bias_rows, head_count, head_size, mask_bias):
    w_qkv, w_out, w_in, w_down = matrices
    normed, norm_one = norm_forward(residual, gain_rows[0], bias_rows[0])
    gathered = gather_rows(normed.astype(jnp.bfloat16))
    attended, stored = attention_forward(gathered, w_qkv, head_count, head_size, mask_bias)
    middle = residual + branch_rows(attended, w_out)
    normed_two, norm_two = norm_forward(middle, gain_rows[1], bias_rows[1])
    gathered_two = gather_rows(normed_two.astype(jnp.bfloat16))
    hidden = jnp.dot(gathered_two, w_in, preferred_element_type=jnp.float32)
    active = jax.nn.gelu(hidden, approximate=False).astype(jnp.bfloat16)
    result = middle + branch_rows(active, w_down)
    return (result, (gathered, norm_one, attended, stored, gathered_two, norm_two, hidden, active))


def block_backward(upstream, matrices, gain_rows, saved_values, head_count, head_size, mask_bias):
    w_qkv, w_out, w_in, w_down = matrices
    gathered, norm_one, attended, stored, gathered_two, norm_two, hidden, active = saved_values
    down_full = gather_grads(upstream.astype(jnp.bfloat16))
    grad_down = inner_rows(active, down_full)
    active_grad = times_transpose(down_full, w_down)
    gelu_pull = jax.vjp(partial(jax.nn.gelu, approximate=False), hidden)[1]
    hidden_grad = gelu_pull(active_grad)[0].astype(jnp.bfloat16)
    grad_in = inner_rows(gathered_two, hidden_grad)
    normed_two_grad = input_rows(hidden_grad, w_in)
    middle_grad, gain_two, bias_two = norm_backward(normed_two_grad, norm_two, gain_rows[1])
    middle_grad = upstream + middle_grad
    middle_full = gather_grads(middle_grad.astype(jnp.bfloat16))
    projected_grad, grad_out = attention_backward(
        middle_full, w_out, attended, stored, head_count, head_size, mask_bias
    )
    grad_qkv = inner_rows(gathered, projected_grad)
    normed_grad = input_rows(projected_grad, w_qkv)
    input_grad, gain_one, bias_one = norm_backward(normed_grad, norm_one, gain_rows[0])
    return (
        middle_grad + input_grad,
        [grad_qkv, grad_out, grad_in, grad_down],
        (gain_one, gain_two, bias_one, bias_two),
    )


def embed_forward(residual, w_embed):
    residual_low = gather_rows(residual.astype(jnp.bfloat16))
    columns = jnp.dot(residual_low, w_embed, preferred_element_type=jnp.float32).astype(
        jnp.bfloat16
    )
    own_columns = lax.all_to_all(columns, "tensor", split_axis=0, concat_axis=1, tiled=True)
    return (own_columns.astype(jnp.float32), residual_low)


def embed_backward(upstream, residual_low, w_embed):
    columns = lax.all_to_all(
        upstream.astype(jnp.bfloat16), "tensor", split_axis=1, concat_axis=0, tiled=True
    )
    grad_embed = inner_rows(residual_low, columns)
    return (input_rows(columns, w_embed), grad_embed)


def slot_builder(gradients, unit_of_slot, unit_width):
    flat_units = jnp.concatenate([gradient.reshape(-1) for gradient in gradients]).reshape(
        -1, unit_width
    )
    unit_total = flat_units.shape[0]
    source = jnp.take(flat_units, jnp.clip(unit_of_slot, 0, unit_total - 1), axis=0)
    return jnp.where((unit_of_slot >= 0)[:, None], source, 0.0)


def per_device(
    tokens_in,
    positions,
    segment_ids,
    owners,
    master,
    first_moment,
    second_moment,
    norm_gains,
    norm_biases,
    norm_first,
    norm_second,
    cotangent,
):
    devices = lax.axis_size("dp")
    tensor_count = lax.axis_size("tensor")
    capacity = master.shape[0]
    unit_width = master.shape[1]
    unit_count = owners.shape[0]
    slot_index = slot_table(owners, devices, capacity)
    unit_of_slot = (
        jnp.full((devices * capacity,), -1, jnp.int32)
        .at[slot_index]
        .set(jnp.arange(unit_count, dtype=jnp.int32))
    )
    targets = unit_of_slot
    targets = jnp.where(targets < 0, unit_count, targets)
    placed = (
        jnp.zeros((unit_count, unit_width), jnp.bfloat16)
        .at[targets]
        .set(lax.all_gather(master.astype(jnp.bfloat16), "dp", axis=0, tiled=True), mode="drop")
    )
    shapes = weight_shapes(tensor_count)
    matrices = split_flat(placed.reshape(-1), shapes)
    encoder = matrices[0:4]
    w_embed = matrices[4]
    decoder = matrices[5:9]
    enc_heads = HE // tensor_count
    dec_heads = HD // tensor_count
    micro_count = tokens_in.shape[0]
    grad_sums = [jnp.zeros(matrix_shape, jnp.float32) for matrix_shape in shapes]
    norm_sums = jnp.zeros((4, DE + DD), jnp.float32)
    decoded_rows = []
    token_grads = []
    for micro_step in range(micro_count):
        tile_ids = segment_ids[micro_step, 0]
        mask_bias = jnp.where(tile_ids[:, None] == tile_ids[None, :], 0.0, MASK_FILL).astype(
            jnp.float32
        )
        position_now = positions[:, micro_step]
        residual = tokens_in[micro_step].astype(jnp.float32) + sincos_embed(position_now, DE)
        residual, enc_saved = block_forward(
            residual, encoder, norm_gains[:, :DE], norm_biases[:, :DE], enc_heads, HDE, mask_bias
        )
        residual, embed_low = embed_forward(residual, w_embed)
        residual = residual + sincos_embed(position_now, DD)
        residual, dec_saved = block_forward(
            residual, decoder, norm_gains[:, DE:], norm_biases[:, DE:], dec_heads, HDD, mask_bias
        )
        decoded_rows.append(residual)
        upstream, dec_grads, dec_norm = block_backward(
            cotangent[micro_step], decoder, norm_gains[:, DE:], dec_saved, dec_heads, HDD, mask_bias
        )
        upstream, grad_embed = embed_backward(upstream, embed_low, w_embed)
        upstream, enc_grads, enc_norm = block_backward(
            upstream, encoder, norm_gains[:, :DE], enc_saved, enc_heads, HDE, mask_bias
        )
        token_grads.append(upstream)
        step_grads = enc_grads + [grad_embed] + dec_grads
        step_norm = jnp.concatenate([jnp.stack(enc_norm), jnp.stack(dec_norm)], axis=1)
        grad_sums = [total_grad + new_grad for total_grad, new_grad in zip(grad_sums, step_grads)]
        norm_sums = norm_sums + step_norm
    reduced = lax.psum_scatter(
        slot_builder(grad_sums, unit_of_slot, unit_width), "dp", scatter_dimension=0, tiled=True
    )
    norm_total = lax.psum(norm_sums, ("dp", "tensor"))
    new_master, new_first, new_second = adamw(
        master, reduced, first_moment, second_moment, WEIGHT_DECAY, LEARN_RATE
    )
    norm_params = jnp.concatenate([norm_gains, norm_biases], axis=0)
    new_norms, norm_one_new, norm_two_new = adamw(
        norm_params, norm_total, norm_first, norm_second, 0.0, NORM_RATE
    )
    return (
        jnp.stack(decoded_rows),
        jnp.stack(token_grads),
        new_master,
        new_first,
        new_second,
        new_norms,
        norm_one_new,
        norm_two_new,
    )


def solution(mesh):
    return jax.shard_map(
        per_device,
        mesh=mesh,
        in_specs=(
            P(None, ("dp", "tensor"), None),
            P(None, None, ("dp", "tensor")),
            P(None, "dp", None),
            P(),
            P("dp", "tensor"),
            P("dp", "tensor"),
            P("dp", "tensor"),
            P(),
            P(),
            P(),
            P(),
            P(None, ("dp", "tensor"), None),
        ),
        out_specs=(
            P(None, ("dp", "tensor"), None),
            P(None, ("dp", "tensor"), None),
            P("dp", "tensor"),
            P("dp", "tensor"),
            P("dp", "tensor"),
            P(),
            P(),
            P(),
        ),
        check_vma=False,
    )
```

profile of v0, /device:TPU:1, one launch (start us, length us, event | category | flops | bytes accessed | tf_op | source)
XLA Modules:
  0.0 1208.1 jit_solution(6353263152077916387)
XLA Ops:
  7.2 3.0 convert_element_type.453
  10.5 4.9 reduce-window.6
  16.9 48.8 %scatter_custom_fusion = s32[20736]{0:T(1024)S(1)} fusion(s32[10368]{0:T(1024)S(1)} %fusion.139, s32[10368]{0:T(1024)S(1)} %iota.55, s32[]{:T(128)} %constant.62.clone.1), kind=kCustom, calls=%fused_computation.377 | custom fusion | bytes 82948 | tf_op jit(solution)/shard_map/scatter | solution.py:308
  72.0 6.0 all_gather.68
  78.0 4.9 all_gather.72
  84.2 5.6 all_gather.57
  89.8 6.1 all_gather.63
  98.8 24.1 %all-gather.2.cloned.1.call-done = bf16[20736,512]{1,0:T(8,128)(2,1)} async-done(((bf16[1296,512]{1,0:T(8,128)(2,1)}), bf16[20736,512]{1,0:T(8,128)(2,1)}) %all-gather.2.cloned.1.call-update) | async-done | bytes 21233680 | tf_op jit(solution)/shard_map/all_gather | solution.py:315
  123.0 105.8 %scatter_custom_fusion.1 = bf16[10368,512]{1,0:T(8,128)(2,1)} fusion(s32[20736]{0:T(1024)S(1)} %get-tuple-element.95, bf16[20736,512]{1,0:T(8,128)(2,1)} %all-gather.2.cloned.1.call-done, bf16[]{:T(256)} %constant.61.clone.1), kind=kCustom, calls=%fused_computation.4 | custom fusion | bytes 10617344 | tf_op jit(solution)/shard_map/scatter | solution.py:315
  228.8 5.0 fusion.161
  234.2 3.0 reshape.556
  245.9 5.2 reshape.561
  251.1 4.9 reshape.560
  259.6 14.4 %reduce-scatter.28.cloned.1.call-done = bf16[128,768]{1,0:T(8,128)(2,1)} async-done(((bf16[256,768]{1,0:T(8,128)(2,1)}), bf16[128,768]{1,0:T(8,128)(2,1)}) %reduce-scatter.28.cloned.1.call-update) | async-done | bytes 196624 | tf_op jit(solution)/shard_map/reduce_scatter | solution.py:135
  275.8 6.6 all_gather.59
  282.4 5.5 all_gather.64
  287.9 5.1 multiply_convert_fusion.4
  295.8 5.1 multiply_convert_fusion.5
  311.5 6.4 all_gather.65
  319.7 3.5 all-to-all-start.1
  323.2 3.3 reduce-scatter.22.cloned.1.call-done
  327.5 6.4 all_gather.60
  334.8 3.4 all-to-all-start
  343.3 4.5 all_gather.61
  347.8 4.6 all_gather.66
  367.0 10.0 reduce-scatter.24.cloned.1.call-done
  378.9 12.0 reduce-scatter.32.cloned.1.call-done
  394.1 5.2 all_gather.62
  399.2 4.5 all_gather.67
  403.7 3.5 multiply_convert_fusion.6
  410.4 4.6 multiply_convert_fusion.7
  439.9 11.7 reduce-scatter.34.cloned.1.call-done
  451.6 14.6 %reduce-scatter.26.cloned.1.call-done = bf16[128,512]{1,0:T(8,128)(2,1)} async-done(((bf16[256,512]{1,0:T(8,128)(2,1)}), bf16[128,512]{1,0:T(8,128)(2,1)}) %reduce-scatter.26.cloned.1.call-update) | async-done | bytes 131088 | tf_op jit(solution)/shard_map/reduce_scatter | solution.py:135
  468.8 5.2 all_gather.69
  476.2 4.7 all_gather.73
  494.3 3.0 convolution_add_fusion.3
  500.9 6.2 reduce-scatter.38.cloned.1.call-done
  508.8 12.9 %reduce-scatter.48.cloned.1.call-done = bf16[128,512]{1,0:T(8,128)(2,1)} async-done(((bf16[256,512]{1,0:T(8,128)(2,1)}), bf16[128,512]{1,0:T(8,128)(2,1)}) %reduce-scatter.48.cloned.1.call-update) | async-done | bytes 131088 | tf_op jit(solution)/shard_map/reduce_scatter | solution.py:144
  524.2 3.4 all-to-all-start.2
  527.6 3.2 all-to-all-done.2
  532.8 3.4 all-to-all-start.3
  536.6 2.9 all-to-all-done.3
  542.2 4.9 reduce-scatter.40.cloned.1.call-done
  547.2 6.9 all_gather.70
  554.1 3.9 add_convert_fusion.1
  559.6 3.0 fusion.171
  562.6 3.0 fusion.172
  565.7 6.3 all_gather.74
  572.0 3.8 add_convert_fusion
  577.5 5.7 convolution_add_fusion.2
  583.2 5.3 convolution_add_fusion.1
  588.5 5.6 reshape.577
  594.2 5.8 reshape.578
  604.7 5.2 all_gather.71
  612.6 5.2 all_gather.75
  635.6 3.5 convolution_add_fusion
  639.0 4.6 reshape.575
  643.7 4.1 constant_dynamic-update-slice_fusion.8
  662.2 23.4 %reshape.584 = f32[10368,512]{1,0:T(8,128)} reshape(f32[5308416]{0:T(1024)} %constant_dynamic-update-slice_fusion) | data formatting | bytes 42467328 | tf_op jit(solution)/shard_map/reshape | solution.py:277
  687.1 68.9 %gather_fusion = f32[20736,512]{1,0:T(8,128)} fusion(f32[10368,512]{1,0:T(8,128)} %reshape.584, s32[21504]{0:T(1024)S(1)} %copy-done.106), kind=kCustom, calls=%fused_computation | custom fusion | bytes 85017600 | tf_op jit(solution)/shard_map/jit(_take)/gather | solution.py:281
  756.1 28.1 %select_select_fusion = f32[20736,512]{1,0:T(8,128)} fusion(f32[20736,512]{1,0:T(8,128)} %gather_fusion, pred[20736]{0:T(1024)(128)(4,1)S(1)} %copy-done.113, pred[20736]{0:T(1024)(128)(4,1)S(1)} %copy-done.112), kind=kLoop, calls=%fused_computation.3 | loop fusion | flops 21233664 | bytes 84976128 | tf_op jit(solution)/shard_map/jit(_where)/select_n | solution.py:282
  790.3 42.6 %psum.7 = f32[4,1280]{1,0:T(4,128)S(1)} all-reduce(f32[4,1280]{1,0:T(4,128)S(1)} %maximum_add_fusion), channel_id=1, replica_groups=mesh['dp'=16,'tensor'=2] {'dp','tensor'}, use_global_device_ids=true, to_apply=%region_84.85 | all-reduce | flops 5120 | bytes 40960 | tf_op jit(solution)/shard_map/psum | solution.py:360
  837.3 355.5 %reduce-scatter.56.cloned.1.call-done = f32[1296,512]{1,0:T(8,128)} async-done(((f32[20736,512]{1,0:T(8,128)}), f32[1296,512]{1,0:T(8,128)}) %reduce-scatter.56.cloned.1.call-update) | async-done | bytes 2654224 | tf_op jit(solution)/shard_map/reduce_scatter | solution.py:357
  1192.8 8.0 multiply_subtract_fusion
  (600 shorter events, 180.6 us)
Async XLA Ops:
  7.2 115.8 %all-gather.2.cloned.1.call-start = ((), (), s32[]{:S(2)}) async-start(), calls=%async_computation.23 | async-start | bytes 22560768 | tf_op jit(solution)/shard_map/all_gather | solution.py:315
  10.2 248.1 %reduce-scatter.20.cloned.1.call-start = ((), (), s32[]{:S(2)}) async-start(), calls=%async_computation.24 | async-start | bytes 589824 | tf_op jit(solution)/shard_map/reduce_scatter | solution.py:135
  15.4 50.3 %copy-start.151 = (s32[3,2,128]{2,1,0:T(2,128)S(1)}, s32[3,2,128]{2,1,0:T(2,128)}, u32[]{:S(2)}) copy-start(s32[3,2,128]{2,1,0:T(2,128)} %param.13) | copy-start | bytes 9220
  83.7 12.2 %copy-start.10 = (f32[128,768]{1,0:T(8,128)}, f32[128,768]{1,0:T(8,128)S(1)}, u32[]{:S(2)}) copy-start(f32[128,768]{1,0:T(8,128)S(1)} %get-tuple-element.69) | copy-start | bytes 1179652
  83.7 12.2 %copy-start.15 = (f32[128,768]{1,0:T(8,128)}, f32[128,768]{1,0:T(8,128)S(1)}, u32[]{:S(2)}) copy-start(f32[128,768]{1,0:T(8,128)S(1)} %get-tuple-element.89) | copy-start | bytes 1179652
  83.7 12.2 %copy-start.137 = (f32[128]{0:T(128)}, f32[128]{0:T(128)S(1)}, u32[]{:S(2)}) copy-start(f32[128]{0:T(128)S(1)} %broadcast_multiply_fusion.23) | copy-start | bytes 1540
  84.0 13.5 %copy-start.143 = (f32[128]{0:T(128)}, f32[128]{0:T(128)S(1)}, u32[]{:S(2)}) copy-start(f32[128]{0:T(128)S(1)} %add_rsqrt_fusion.3) | copy-start | bytes 1540
  84.0 13.5 %copy-start.145 = (f32[128]{0:T(128)}, f32[128]{0:T(128)S(1)}, u32[]{:S(2)}) copy-start(f32[128]{0:T(128)S(1)} %add_rsqrt_fusion.7) | copy-start | bytes 1540
  96.6 148.6 %copy-start.50 = (f32[256,256]{0,1:T(8,128)}, f32[256,256]{0,1:T(8,128)S(1)}, u32[]{:S(2)}) copy-start(f32[256,256]{0,1:T(8,128)S(1)} %compare_select_fusion) | copy-start | bytes 786436
  234.2 22.2 %copy-start.8 = (bf16[384,768]{1,0:T(8,128)(2,1)}, bf16[384,768]{1,0:T(8,128)(2,1)S(1)}, u32[]{:S(2)}) copy-start(bf16[384,768]{1,0:T(8,128)(2,1)S(1)} %reshape.559) | copy-start | bytes 1769476
  239.7 16.3 %copy-start.32 = (bf16[256,1152]{0,1:T(8,128)(2,1)}, bf16[256,1152]{0,1:T(8,128)(2,1)S(1)}, u32[]{:S(2)}) copy-start(bf16[256,1152]{0,1:T(8,128)(2,1)S(1)} %copy.90) | copy-start | bytes 1769476
  245.1 28.9 %reduce-scatter.28.cloned.1.call-start = ((), (), s32[]{:S(2)}) async-start(), calls=%async_computation.28 | async-start | bytes 589824 | tf_op jit(solution)/shard_map/reduce_scatter | solution.py:135
  256.4 17.6 %copy-start.16 = (f32[128,768]{1,0:T(8,128)S(1)}, f32[128,768]{1,0:T(8,128)}, u32[]{:S(2)}) copy-start(f32[128,768]{1,0:T(8,128)} %copy-done.15) | copy-start | bytes 1179652
  258.2 17.1 %copy-start.110 = (f32[768]{0:T(1024)S(1)}, f32[768]{0:T(1024)}, u32[]{:S(2)}) copy-start(f32[768]{0:T(1024)} %get-tuple-element.191) | copy-start | bytes 9220
  258.3 17.1 %copy-start.122 = (f32[768]{0:T(1024)S(1)}, f32[768]{0:T(1024)}, u32[]{:S(2)}) copy-start(f32[768]{0:T(1024)} %get-tuple-element.42) | copy-start | bytes 9220
  258.3 52.3 %reduce-scatter.30.cloned.1.call-start = ((), (), s32[]{:S(2)}) async-start(), calls=%async_computation.29 | async-start | bytes 589824 | tf_op jit(solution)/shard_map/reduce_scatter | solution.py:135
  259.4 23.0 %copy-start.13 = (f32[128,768]{1,0:T(8,128)}, f32[128,768]{1,0:T(8,128)S(1)}, u32[]{:S(2)}) copy-start(f32[128,768]{1,0:T(8,128)S(1)} %get-tuple-element.67) | copy-start | bytes 1179652
  259.4 16.1 %copy-start.141 = (f32[128]{0:T(128)}, f32[128]{0:T(128)S(1)}, u32[]{:S(2)}) copy-start(f32[128]{0:T(128)S(1)} %broadcast_multiply_fusion.22) | copy-start | bytes 1540
  259.6 15.9 %copy-start.149 = (f32[128]{0:T(128)}, f32[128]{0:T(128)S(1)}, u32[]{:S(2)}) copy-start(f32[128]{0:T(128)S(1)} %add_rsqrt_fusion.6) | copy-start | bytes 1540
  275.1 18.0 %copy-start.18 = (f32[128,768]{1,0:T(8,128)}, f32[128,768]{1,0:T(8,128)S(1)}, u32[]{:S(2)}) copy-start(f32[128,768]{1,0:T(8,128)S(1)} %get-tuple-element.79) | copy-start | bytes 1179652
  275.1 12.8 %copy-start.52 = (bf16[768,1536]{1,0:T(8,128)(2,1)S(1)}, bf16[768,1536]{1,0:T(8,128)(2,1)}, u32[]{:S(2)}) copy-start(bf16[768,1536]{1,0:T(8,128)(2,1)} %reshape.560) | copy-start | bytes 7077892
  282.4 13.4 %copy-start.67 = (bf16[256,768]{1,0:T(8,128)(2,1)}, bf16[256,768]{1,0:T(8,128)(2,1)S(1)}, u32[]{:S(2)}) copy-start(bf16[256,768]{1,0:T(8,128)(2,1)S(1)} %all_gather.59) | copy-start | bytes 1179652
  295.5 31.0 %reduce-scatter.22.cloned.1.call-start = ((), (), s32[]{:S(2)}) async-start(), calls=%async_computation.25 | async-start | bytes 589824 | tf_op jit(solution)/shard_map/reduce_scatter | solution.py:135
  306.6 47.8 %copy-start.6 = (bf16[512,768]{1,0:T(8,128)(2,1)}, bf16[512,768]{1,0:T(8,128)(2,1)S(1)}, u32[]{:S(2)}) copy-start(bf16[512,768]{1,0:T(8,128)(2,1)S(1)} %reshape.563) | copy-start | bytes 2359300
  306.6 12.2 %copy-start.21 = (bf16[768,256]{1,0:T(8,128)(2,1)S(1)}, bf16[768,256]{1,0:T(8,128)(2,1)}, u32[]{:S(2)}) copy-start(bf16[768,256]{1,0:T(8,128)(2,1)} %reshape.562) | copy-start | bytes 1179652
  307.7 18.8 %copy-start.14 = (f32[128,768]{1,0:T(8,128)S(1)}, f32[128,768]{1,0:T(8,128)}, u32[]{:S(2)}) copy-start(f32[128,768]{1,0:T(8,128)} %copy-done.13) | copy-start | bytes 1179652
  319.7 18.6 %copy-start.37 = (f32[128,512]{1,0:T(8,128)S(1)}, f32[128,512]{1,0:T(8,128)}, u32[]{:S(2)}) copy-start(f32[128,512]{1,0:T(8,128)} %concatenate.32) | copy-start | bytes 786436
  319.7 15.1 %all-to-all-start.1 = ((bf16[2,128,256]{2,1,0:T(8,128)(2,1)}), bf16[2,128,256]{2,1,0:T(8,128)(2,1)S(1)}, u32[]{:S(2)}, u32[]{:S(2)}) async-start(bf16[2,128,256]{2,1,0:T(8,128)(2,1)} %bitcast.36), calls=%async_computation.7 | async-start | bytes 262144 | tf_op jit(solution)/shard_map/all_to_all | solution.py:264
  334.8 6.7 all-to-all-start
  338.2 38.8 %reduce-scatter.24.cloned.1.call-start = ((), (), s32[]{:S(2)}) async-start(), calls=%async_computation.26 | async-start | bytes 393216 | tf_op jit(solution)/shard_map/reduce_scatter | solution.py:135
  360.9 30.1 %reduce-scatter.32.cloned.1.call-start = ((), (), s32[]{:S(2)}) async-start(), calls=%async_computation.30 | async-start | bytes 393216 | tf_op jit(solution)/shard_map/reduce_scatter | solution.py:135
  364.4 28.6 %copy-start.119 = (f32[1,512]{1,0:T(1,128)S(1)}, f32[1,512]{1,0:T(1,128)}, u32[]{:S(2)}) copy-start(f32[1,512]{1,0:T(1,128)} %get-tuple-element.96) | copy-start | bytes 6148
  366.9 70.2 %reduce-scatter.46.cloned.1.call-start = ((), (), s32[]{:S(2)}) async-start(), calls=%async_computation.37 | async-start | bytes 393216 | tf_op jit(solution)/shard_map/reduce_scatter | solution.py:144
  391.0 12.7 %copy-start.22 = (bf16[512,1024]{1,0:T(8,128)(2,1)S(1)}, bf16[512,1024]{1,0:T(8,128)(2,1)}, u32[]{:S(2)}) copy-start(bf16[512,1024]{1,0:T(8,128)(2,1)} %reshape.566) | copy-start | bytes 3145732
  391.0 16.3 %slice-start = ((s8[10616832]{0:T(1024)(128)(4,1)}), s8[4194304]{0:T(1024)(128)(4,1)S(1)}, s32[]{:S(2)}) async-start(s8[10616832]{0:T(1024)(128)(4,1)} %bitcast.403), calls=%async_computation.43 | async-start | bytes 8388608
  410.0 27.9 %reduce-scatter.36.cloned.1.call-start = ((), (), s32[]{:S(2)}) async-start(), calls=%async_computation.32 | async-start | bytes 393216 | tf_op jit(solution)/shard_map/reduce_scatter | solution.py:144
  422.0 29.6 %reduce-scatter.34.cloned.1.call-start = ((), (), s32[]{:S(2)}) async-start(), calls=%async_computation.31 | async-start | bytes 393216 | tf_op jit(solution)/shard_map/reduce_scatter | solution.py:135
  427.5 38.7 %reduce-scatter.26.cloned.1.call-start = ((), (), s32[]{:S(2)}) async-start(), calls=%async_computation.27 | async-start | bytes 393216 | tf_op jit(solution)/shard_map/reduce_scatter | solution.py:135
  437.1 70.0 %reduce-scatter.38.cloned.1.call-start = ((), (), s32[]{:S(2)}) async-start(), calls=%async_computation.33 | async-start | bytes 393216 | tf_op jit(solution)/shard_map/reduce_scatter | solution.py:144
  468.8 13.4 %copy-start.1 = (f32[8,256,256]{1,2,0:T(8,128)S(1)}, f32[8,256,256]{1,2,0:T(8,128)}, u32[]{:S(2)}) copy-start(f32[8,256,256]{1,2,0:T(8,128)} %copy-done) | copy-start | bytes 6291460
  493.3 28.4 %reduce-scatter.48.cloned.1.call-start = ((), (), s32[]{:S(2)}) async-start(), calls=%async_computation.38 | async-start | bytes 393216 | tf_op jit(solution)/shard_map/reduce_scatter | solution.py:144
  499.8 21.9 %copy-start.36 = (f32[128,512]{1,0:T(8,128)S(1)}, f32[128,512]{1,0:T(8,128)}, u32[]{:S(2)}) copy-start(f32[128,512]{1,0:T(8,128)} %get-tuple-element.112) | copy-start | bytes 786436
  499.8 21.9 %copy-start.94 = (f32[128,512]{1,0:T(8,128)S(1)}, f32[128,512]{1,0:T(8,128)}, u32[]{:S(2)}) copy-start(f32[128,512]{1,0:T(8,128)} %get-tuple-element.53) | copy-start | bytes 786436
  508.8 23.2 %copy-start.88 = (f32[128,512]{1,0:T(8,128)S(1)}, f32[128,512]{1,0:T(8,128)}, u32[]{:S(2)}) copy-start(f32[128,512]{1,0:T(8,128)} %get-tuple-element.85) | copy-start | bytes 786436
  523.5 12.7 %copy-start.45 = (bf16[256,768]{1,0:T(8,128)(2,1)S(1)}, bf16[256,768]{1,0:T(8,128)(2,1)}, u32[]{:S(2)}) copy-start(bf16[256,768]{1,0:T(8,128)(2,1)} %copy-done.44) | copy-start | bytes 1179652
  524.2 6.7 all-to-all-start.2
  527.6 19.6 %reduce-scatter.40.cloned.1.call-start = ((), (), s32[]{:S(2)}) async-start(), calls=%async_computation.34 | async-start | bytes 589824 | tf_op jit(solution)/shard_map/reduce_scatter | solution.py:144
  532.8 6.7 all-to-all-start.3
  536.2 29.5 %reduce-scatter.50.cloned.1.call-start = ((), (), s32[]{:S(2)}) async-start(), calls=%async_computation.39 | async-start | bytes 589824 | tf_op jit(solution)/shard_map/reduce_scatter | solution.py:144
  542.2 57.8 %reduce-scatter.42.cloned.1.call-start = ((), (), s32[]{:S(2)}) async-start(), calls=%async_computation.35 | async-start | bytes 589824 | tf_op jit(solution)/shard_map/reduce_scatter | solution.py:144
  565.6 36.3 %reduce-scatter.52.cloned.1.call-start = ((), (), s32[]{:S(2)}) async-start(), calls=%async_computation.40 | async-start | bytes 589824 | tf_op jit(solution)/shard_map/reduce_scatter | solution.py:144
  583.1 203.1 %reduce-scatter.44.cloned.1.call-start = ((), (), s32[]{:S(2)}) async-start(), calls=%async_computation.36 | async-start | bytes 589824 | tf_op jit(solution)/shard_map/reduce_scatter | solution.py:144
  633.3 154.2 %reduce-scatter.54.cloned.1.call-start = ((), (), s32[]{:S(2)}) async-start(), calls=%async_computation.41 | async-start | bytes 589824 | tf_op jit(solution)/shard_map/reduce_scatter | solution.py:144
  662.2 23.4 %copy-start.62 = (bf16[256,3,6,64]{0,3,2,1:T(8,128)(2,1)S(1)}, bf16[256,3,6,64]{0,3,2,1:T(8,128)(2,1)}, u32[]{:S(2)}) copy-start(bf16[256,3,6,64]{0,3,2,1:T(8,128)(2,1)} %copy-done.61) | copy-start | bytes 1769476
  662.2 23.4 %copy-start.74 = (bf16[768,1152]{1,0:T(8,128)(2,1)S(1)}, bf16[768,1152]{1,0:T(8,128)(2,1)}, u32[]{:S(2)}) copy-start(bf16[768,1152]{1,0:T(8,128)(2,1)} %reshape.556) | copy-start | bytes 5308420
  687.1 69.0 %copy-start.112 = (pred[20736]{0:T(1024)(128)(4,1)S(1)}, pred[20736]{0:T(1024)(128)(4,1)}, u32[]{:S(2)}) copy-start(pred[20736]{0:T(1024)(128)(4,1)} %get-tuple-element.92) | copy-start | bytes 62212
  687.1 69.0 %copy-start.113 = (pred[20736]{0:T(1024)(128)(4,1)S(1)}, pred[20736]{0:T(1024)(128)(4,1)}, u32[]{:S(2)}) copy-start(pred[20736]{0:T(1024)(128)(4,1)} %get-tuple-element.93) | copy-start | bytes 62212
  687.1 505.7 %reduce-scatter.56.cloned.1.call-start = ((), (), s32[]{:S(2)}) async-start(), calls=%async_computation.42 | async-start | bytes 45121536 | tf_op jit(solution)/shard_map/reduce_scatter | solution.py:357
  790.1 45.6 %copy-start.81 = (f32[1,128,768]{2,1,0:T(8,128)S(1)}, f32[1,128,768]{2,1,0:T(8,128)}, u32[]{:S(2)}) copy-start(f32[1,128,768]{2,1,0:T(8,128)} %get-tuple-element.104) | copy-start | bytes 1179652
  790.1 46.5 %copy-start.116 = (f32[2,1280]{1,0:T(2,128)S(1)}, f32[2,1280]{1,0:T(2,128)}, u32[]{:S(2)}) copy-start(f32[2,1280]{1,0:T(2,128)} %param.20) | copy-start | bytes 30724
  790.1 46.5 %copy-start.118 = (f32[2,1280]{1,0:T(2,128)S(1)}, f32[2,1280]{1,0:T(2,128)}, u32[]{:S(2)}) copy-start(f32[2,1280]{1,0:T(2,128)} %param.19) | copy-start | bytes 30724
  790.1 46.5 %copy-start.120 = (f32[4,1280]{1,0:T(4,128)S(1)}, f32[4,1280]{1,0:T(4,128)}, u32[]{:S(2)}) copy-start(f32[4,1280]{1,0:T(4,128)} %param.21) | copy-start | bytes 61444
  790.1 46.5 %copy-start.121 = (f32[4,1280]{1,0:T(4,128)S(1)}, f32[4,1280]{1,0:T(4,128)}, u32[]{:S(2)}) copy-start(f32[4,1280]{1,0:T(4,128)} %param.22) | copy-start | bytes 61444
  790.3 402.5 %copy-start.20 = (f32[1296,512]{1,0:T(8,128)S(1)}, f32[1296,512]{1,0:T(8,128)}, u32[]{:S(2)}) copy-start(f32[1296,512]{1,0:T(8,128)} %param.16) | copy-start | bytes 7962628
  (125 other events, 443.3 us)
Sparse Core Ops, SparseCore 0:
  10.3 112.5 all-gather.1
  245.3 12.6 reduce-scatter.19
  260.9 13.1 reduce-scatter.27
  295.6 14.9 reduce-scatter.29
  313.3 13.1 reduce-scatter.21
  361.0 15.9 reduce-scatter.23
  379.3 11.6 reduce-scatter.31
  410.1 13.6 reduce-scatter.45
  426.1 11.6 reduce-scatter.35
  439.9 11.6 reduce-scatter.33
  454.5 11.6 reduce-scatter.25
  493.4 13.6 reduce-scatter.37
  510.0 11.6 reduce-scatter.47
  532.1 15.0 reduce-scatter.39
  549.4 12.8 reduce-scatter.49
  565.7 13.6 reduce-scatter.41
  583.3 14.4 reduce-scatter.51
  633.4 16.7 reduce-scatter.43
  687.2 16.7 reduce-scatter.53
  784.4 408.3 reduce-scatter.55
where the time goes:
time: 1220 us; the launch traced here: 1210 us
  waiting for transfers between devices  482 us (40%)
  local copies, waits for them, and re-layouts  337 us (28%)
  blocking collectives  142 us (12%)
  matrix products  125 us (10%)
  other arithmetic  89.9 us (7%)
  between operations  17 us (1%)
  starting transfers between devices  15.3 us (1%)
    reduce_scatter x1, waiting for transfers between devices, per_device(): lax.psum_scatter(slot_builder(grad_sums, unit_of_slot, unit_width), 'dp',...  356 us
    scatter x1, local copies, waits for them, and re-layouts, per_device(): placed = jnp.zeros((unit_count, unit_width), jnp.bfloat16).at[targets].se...  106 us
    gather x1, local copies, waits for them, and re-layouts, slot_builder(): jnp.take(flat_units, jnp.clip(unit_of_slot, 0, unit_total - 1), axis=0)  68.9 us
    reduce_scatter x8, waiting for transfers between devices, branch_rows(): lax.psum_scatter(jnp.dot(values, weight, preferred_element_type=jnp.float...  68.9 us
    all_gather x10, blocking collectives, gather_rows(): return lax.all_gather(values, 'tensor', axis=0, tiled=True)  55.3 us
    scatter x1, local copies, waits for them, and re-layouts, per_device(): unit_of_slot = jnp.full((devices * capacity,), -1, jnp.int32).at[slot_ind...  48.8 us
    all_gather x8, blocking collectives, gather_grads(): return lax.all_gather(values, 'tensor', axis=0, tiled=True)  44.3 us
    psum x1, blocking collectives, per_device(): norm_total = lax.psum(norm_sums, ('dp', 'tensor'))  42.6 us
  transfers between devices with their start and end apart: 24, of which 16 were waited for; matrix products, arithmetic and copies ran while one was open for 28% of the time, Pallas kernels for 0%

commit v1 on v0

--- a/solution.py
+++ b/solution.py
@@ -3,6 +3,8 @@
 import jax
 import jax.numpy as jnp
 from jax import lax
+from jax.experimental import pallas as pl
+from jax.experimental.pallas import tpu as pltpu
 from jax.sharding import PartitionSpec as P
 
 DE = 768
@@ -377,9 +379,487 @@
     )
 
 
+MESH = pl.DeviceIdType.MESH
+ALL = slice(None)
+
+
+class Place:
+    def __init__(self):
+        self.d = lax.axis_index("dp")
+        self.x = lax.axis_index("tensor")
+        self.z = self.d // 4
+        self.y = (self.d // 2) % 2
+        self.c = self.d % 2
+        self.ids = {
+            "c": (self.d + 1 - 2 * self.c, self.x),
+            "y": (self.d + 2 - 4 * self.y, self.x),
+            "x": (self.d, 1 - self.x),
+            "z+": (self.d + 4, self.x),
+            "z-": (self.d - 4, self.x),
+        }
+
+    def greet(self, kinds):
+        bar = pltpu.get_barrier_semaphore()
+        for k in kinds:
+            pl.semaphore_signal(bar, inc=1, device_id=self.ids[k], device_id_type=MESH)
+
+        @pl.when(self.z < 3)
+        def _():
+            pl.semaphore_signal(bar, inc=1, device_id=self.ids["z+"], device_id_type=MESH)
+
+        @pl.when(self.z > 0)
+        def _():
+            pl.semaphore_signal(bar, inc=1, device_id=self.ids["z-"], device_id_type=MESH)
+
+        inner = jnp.where(jnp.logical_and(self.z > 0, self.z < 3), 1, 0)
+        pl.semaphore_wait(bar, len(kinds) + 1 + inner)
+
+    def there(self, disp):
+        dz = disp[0]
+        if dz == 0:
+            return None
+        return self.z + dz <= 3 if dz > 0 else self.z + dz >= 0
+
+    def at(self, disp):
+        dz, fy, fx = disp
+        return (1 - self.x if fx else self.x, self.z + dz, 1 - self.y if fy else self.y)
+
+
+def when(cond, f):
+    if cond is None:
+        f()
+    else:
+        pl.when(cond)(f)
+
+
+def both(a, b):
+    if a is None:
+        return b
+    if b is None:
+        return a
+    return jnp.logical_and(a, b)
+
+
+def spread(order):
+    out = {}
+    todo = [((0, 0, 0), -1, 0)]
+    while todo:
+        (dz, fy, fx), last, way = todo.pop(0)
+        nxt = []
+        for i, a in enumerate(order):
+            if i < last:
+                continue
+            if a == "z":
+                for s in (1, -1):
+                    if i == last and s != way:
+                        continue
+                    n = (dz - s, fy, fx)
+                    if abs(n[0]) <= 3:
+                        nxt.append((n, "z+" if s > 0 else "z-", i, s))
+            elif i > last:
+                n = (dz, 1, fx) if a == "y" else (dz, fy, 1)
+                nxt.append((n, a, i, 0))
+        out[(dz, fy, fx)] = [(n, w) for n, w, _, _ in nxt]
+        todo += [(n, i, s) for n, _, i, s in nxt]
+    return out
+
+
+def hops(d):
+    return abs(d[0]) + d[1] + d[2]
+
+
+BACK = {"z+": "z-", "z-": "z+", "x": "x", "y": "y"}
+
+
+def gather_kernel(plan, with_x, mine, out, send, recv, sib_send, sib_recv, own_sem):
+    p = Place()
+    p.greet(["c", "y", "x"] if with_x else ["c", "y"])
+    trees = [spread(o) for o, _, _ in plan]
+    ids = [{d: i + 32 * g for i, d in enumerate(sorted(t))} for g, t in enumerate(trees)]
+    waits = []
+
+    def at(disp, core, g):
+        t, z, y = p.at(disp)
+        return out.at[((t,) if with_x else ()) + (z, y, core, pl.ds(plan[g][1], plan[g][2]))]
+
+    def push(src, g, nd, way, cond):
+        k = ids[g][nd]
+        od = None
+        cp = pltpu.make_async_remote_copy(src_ref=src[0], dst_ref=src[1], send_sem=send.at[k], recv_sem=recv.at[k],
+                                          device_id=p.ids[way], device_id_type=MESH)
+        c2 = cond
+        if way == "z+":
+            c2 = both(cond, p.z < 3)
+        elif way == "z-":
+            c2 = both(cond, p.z > 0)
+        when(c2, cp.start)
+        waits.append((c2, cp))
+
+    def share(src, g, disp, cond):
+        k = ids[g][disp]
+        cp = pltpu.make_async_remote_copy(src_ref=src, dst_ref=at(disp, p.c, g), send_sem=sib_send.at[k], recv_sem=sib_recv.at[k],
+                                          device_id=p.ids["c"], device_id_type=MESH)
+        when(cond, cp.start)
+        waits.append((cond, cp))
+
+    zero = (0, 0, 0)
+    for g, tree in enumerate(trees):
+        src = mine.at[pl.ds(plan[g][1], plan[g][2])]
+        for nd, way in tree[zero]:
+            push((src, at(zero, p.c, g)), g, nd, way, None)
+    own = pltpu.make_async_copy(mine, out.at[((p.x,) if with_x else ()) + (p.z, p.y, p.c)], own_sem)
+    own.start()
+    for g in range(len(plan)):
+        share(mine.at[pl.ds(plan[g][1], plan[g][2])], g, zero, None)
+    events = sorted((hops(d), g, d) for g, t in enumerate(trees) for d in t if d != zero)
+    for _, g, d in events:
+        cond = p.there(d)
+        blk = at(d, p.c, g)
+        got = pltpu.make_async_remote_copy(src_ref=blk, dst_ref=blk, send_sem=send.at[ids[g][d]], recv_sem=recv.at[ids[g][d]],
+                                           device_id=p.ids["c"], device_id_type=MESH)
+        when(cond, got.wait_recv)
+        for nd, way in trees[g][d]:
+            push((blk, blk), g, nd, way, cond)
+        share(blk, g, d, cond)
+    for g, t in enumerate(trees):
+        for d in t:
+            blk = at(d, 1 - p.c, g)
+            got = pltpu.make_async_remote_copy(src_ref=blk, dst_ref=blk, send_sem=sib_send.at[ids[g][d]], recv_sem=sib_recv.at[ids[g][d]],
+                                               device_id=p.ids["c"], device_id_type=MESH)
+            when(p.there(d), got.wait_recv)
+    own.wait()
+    for c, cp in waits:
+        when(c, cp.wait_send)
+
+
+def gather(shard, plan, with_x, ident, space=pl.ANY):
+    rows, width = shard.shape
+    lead = (2, 4, 2, 2) if with_x else (4, 2, 2)
+    sems = pltpu.SemaphoreType.DMA((32 * len(plan),))
+    return pl.pallas_call(
+        partial(gather_kernel, plan, with_x),
+        out_shape=jax.ShapeDtypeStruct(lead + (rows, width), shard.dtype),
+        in_specs=[pl.BlockSpec(memory_space=space)],
+        out_specs=pl.BlockSpec(memory_space=space),
+        scratch_shapes=[sems, sems, sems, sems, pltpu.SemaphoreType.DMA],
+        compiler_params=pltpu.CompilerParams(collective_id=ident, has_side_effects=True, vmem_limit_bytes=60 << 20),
+        name=f"gather_{ident}",
+    )(shard)
+
+
+def add_rows(acc, got, step=80):
+    n = acc.shape[0]
+    while n % step:
+        step -= 16
+
+    def body(i, _):
+        r = pl.ds(pl.multiple_of(i * step, step), step)
+        acc[r, :] = acc[r, :] + got[r, :]
+        return 0
+
+    lax.fori_loop(0, n // step, body, 0)
+
+
+def reduce_kernel(plan, with_x, src, out, *rest):
+    n = len(plan)
+    accs, halves, bufs = rest[:n], rest[n:2 * n], rest[2 * n:3 * n]
+    send, recv, sib_send, sib_recv, loads = rest[3 * n:]
+    p = Place()
+    p.greet(["c", "y", "x"] if with_x else ["c", "y"])
+    trees = [spread(o) for o, _, _ in plan]
+    ids = [{d: i + 32 * g for i, d in enumerate(sorted(t))} for g, t in enumerate(trees)]
+    waits = []
+    zero = (0, 0, 0)
+
+    def ix(disp):
+        t, z, y = p.at(disp)
+        return ((t,) if with_x else ()) + (z, y)
+
+    events = sorted((-hops(d), g, d) for g, t in enumerate(trees) for d in t)
+    for _, g, d in events:
+        cond = p.there(d)
+        k = ids[g][d]
+        rows = pl.ds(plan[g][1], plan[g][2])
+        cp = pltpu.make_async_remote_copy(
+            src_ref=src.at[ix(d) + (1 - p.c, rows)], dst_ref=halves[g].at[ix(d)], send_sem=sib_send.at[k],
+            recv_sem=sib_recv.at[k], device_id=p.ids["c"], device_id_type=MESH)
+        ld = pltpu.make_async_copy(src.at[ix(d) + (p.c, rows)], accs[g].at[ix(d)], loads.at[k])
+
+        def go(cp=cp, ld=ld):
+            cp.start()
+            ld.start()
+        when(cond, go)
+        waits.append((cond, cp))
+    for _, g, d in events:
+        k = ids[g][d]
+        rows = pl.ds(plan[g][1], plan[g][2])
+        base = k - ids[g][min(trees[g])]
+
+        def step(g=g, d=d, k=k, rows=rows):
+            acc = accs[g].at[ix(d)]
+            pltpu.make_async_copy(src.at[ix(d) + (p.c, rows)], acc, loads.at[k]).wait()
+            half = halves[g].at[ix(d)]
+            pltpu.make_async_remote_copy(src_ref=half, dst_ref=half, send_sem=sib_send.at[k], recv_sem=sib_recv.at[k],
+                                         device_id=p.ids["c"], device_id_type=MESH).wait_recv()
+            add_rows(acc, half)
+            for nd, way in trees[g][d]:
+                kk = ids[g][nd]
+                buf = bufs[g].at[kk - 32 * g]
+
+                def take(acc=acc, buf=buf, kk=kk):
+                    pltpu.make_async_remote_copy(src_ref=buf, dst_ref=buf, send_sem=send.at[kk], recv_sem=recv.at[kk],
+                                                 device_id=p.ids["c"], device_id_type=MESH).wait_recv()
+                    add_rows(acc, buf)
+                if way == "z+":
+                    when(p.z < 3, take)
+                elif way == "z-":
+                    when(p.z > 0, take)
+                else:
+                    take()
+        cond = p.there(d)
+        when(cond, step)
+        if d != zero:
+            way = [w for t in trees[g].values() for nd, w in t if nd == d][0]
+            acc = accs[g].at[ix(d)]
+            cp = pltpu.make_async_remote_copy(src_ref=acc, dst_ref=bufs[g].at[k - 32 * g], send_sem=send.at[k], recv_sem=recv.at[k],
+                                              device_id=p.ids[BACK[way]], device_id_type=MESH)
+            when(cond, cp.start)
+            waits.append((cond, cp))
+        else:
+            out[rows, :] = accs[g][ix(d)]
+    for c, cp in waits:
+        when(c, cp.wait_send)
+
+
+def reduce_scatter(whole, plan, with_x, ident, limit=62 << 20):
+    rows, width = whole.shape[-2:]
+    dt = whole.dtype
+    lead = (2, 4, 2) if with_x else (4, 2)
+    blocks = [pltpu.VMEM(lead + (num, width), dt) for _, _, num in plan]
+    bufs = [pltpu.VMEM((len(spread(o)), num, width), dt) for o, _, num in plan]
+    sems = pltpu.SemaphoreType.DMA((32 * len(plan),))
+    return pl.pallas_call(
+        partial(reduce_kernel, plan, with_x),
+        out_shape=jax.ShapeDtypeStruct((rows, width), dt),
+        in_specs=[pl.BlockSpec(memory_space=pl.ANY)],
+        out_specs=pl.BlockSpec(memory_space=pltpu.VMEM),
+        scratch_shapes=blocks + blocks + bufs + [sems] * 5,
+        compiler_params=pltpu.CompilerParams(collective_id=ident, has_side_effects=True, vmem_limit_bytes=limit),
+        name=f"reduce_{ident}",
+    )(whole)
+
+
+PLAN_ALL = [("zxy", 0, 640), ("zyx", 640, 640), ("xzy", 1280, 640), ("yzx", 1920, 720)]
+PLAN_DP = [("zy", 0, 656)]
+SHARD_UNITS = 656
+PANEL = 128
+
+
+def layout(shapes, shards):
+    table = []
+    unit_at, row_at = 0, 0
+    for rows, cols in shapes:
+        rb, panels = rows // shards, cols // PANEL
+        units = rb * cols // 512
+        padded = -(-rb // 16) * 16
+        table.append((rb, panels, units, unit_at, row_at, padded))
+        unit_at += units
+        row_at += padded * panels
+    return table, unit_at, row_at
+
+
+def unit_places(units, table, shards):
+    place = jnp.zeros_like(units)
+    for rb, panels, n, first, _, _ in table:
+        lo = first * shards
+        v = units - lo
+        here = (v // n) * SHARD_UNITS + first + v % n
+        place = jnp.where(v >= 0, here, place)
+    return place
+
+
+def own_units(owners, mine, capacity):
+    count = owners.shape[0] // 128
+    hit = (owners[:, 0] == mine).reshape(count, 128)
+    lane = jnp.arange(128)
+    tri = (lane[:, None] <= lane[None, :]).astype(jnp.bfloat16)
+    within = jnp.dot(hit.astype(jnp.bfloat16), tri, preferred_element_type=jnp.float32)
+    totals = within[:, 127].astype(jnp.int32)
+    upto = jnp.sum(jnp.where(jnp.arange(count)[:, None] >= jnp.arange(count)[None, :], totals[None, :], 0), axis=1)
+    slot = jnp.arange(capacity, dtype=jnp.int32)
+    block = jnp.sum((upto[None, :] <= slot[:, None]).astype(jnp.int32), axis=1)
+    pick = block[:, None] == jnp.arange(count)[None, :]
+    before = jnp.sum(jnp.where(pick, (upto - totals)[None, :], 0), axis=1)
+    row = jnp.dot(pick.astype(jnp.bfloat16), within.astype(jnp.bfloat16), preferred_element_type=jnp.float32)
+    rank = (slot - before).astype(jnp.float32)
+    at = jnp.sum((row <= rank[:, None]).astype(jnp.int32), axis=1)
+    return block * 128 + at, slot < upto[count - 1]
+
+
+def to_panels(shard, table):
+    out = []
+    for rb, panels, n, first, _, padded in table:
+        m = shard[first:first + n].reshape(rb, panels, PANEL).transpose(1, 0, 2)
+        if padded > rb:
+            m = jnp.pad(m, ((0, 0), (0, padded - rb), (0, 0)))
+        out.append(m.reshape(panels * padded, PANEL))
+    return jnp.concatenate(out, axis=0)
+
+
+def from_panels(rows, table):
+    out = []
+    for rb, panels, n, first, at, padded in table:
+        m = rows[at:at + panels * padded].reshape(panels, padded, PANEL)[:, :rb]
+        out.append(m.transpose(1, 0, 2).reshape(n, 512))
+    out = jnp.concatenate(out, axis=0)
+    return jnp.pad(out, ((0, SHARD_UNITS - out.shape[0]), (0, 0)))
+
+
+BY_ROWS = (1, 3, 6, 8)
+
+
+def unpack(full, table):
+    full = full.reshape(2, 16, full.shape[-2], PANEL)
+    mats = []
+    for i, (rb, panels, n, _, at, padded) in enumerate(table):
+        m = full[:, :, at:at + panels * padded].reshape(2, 16, panels, padded, PANEL)[:, :, :, :rb]
+        if i in BY_ROWS:
+            m = m.transpose(0, 1, 3, 2, 4).reshape(2 * 16 * rb, panels * PANEL)
+        else:
+            m = m.transpose(1, 3, 0, 2, 4).reshape(16 * rb, 2 * panels * PANEL)
+        mats.append(m)
+    return mats
+
+
+def pack(mats, table):
+    out = []
+    for i, (rb, panels, n, _, at, padded) in enumerate(table):
+        m = mats[i].astype(jnp.bfloat16)
+        if i in BY_ROWS:
+            m = m.reshape(2, 16, rb, panels, PANEL).transpose(0, 1, 3, 2, 4)
+        else:
+            m = m.reshape(16, rb, 2, panels, PANEL).transpose(2, 0, 3, 1, 4)
+        if padded > rb:
+            m = jnp.pad(m, ((0, 0), (0, 0), (0, 0), (0, padded - rb), (0, 0)))
+        out.append(m.reshape(2, 16, panels * padded, PANEL))
+    out = jnp.concatenate(out, axis=2)
+    return out.reshape(2, 4, 2, 2, out.shape[2], PANEL)
+
+
+def whole_attention(n1, w_qkv, heads, size, mask):
+    length = n1.shape[0]
+    proj = jnp.dot(n1, w_qkv, preferred_element_type=jnp.float32).astype(jnp.bfloat16)
+    proj = proj.reshape(length, 2, 3, heads // 2, size)
+    q, k, v = (proj[:, :, i].reshape(length, heads, size) for i in range(3))
+    z = jnp.einsum("qhd,khd->hqk", q, k, preferred_element_type=jnp.float32) * size ** (-0.5) + mask[None]
+    e = jnp.exp(z - jnp.max(z, axis=-1, keepdims=True))
+    p = e / jnp.sum(e, axis=-1, keepdims=True)
+    a = jnp.einsum("hqk,khd->qhd", p.astype(jnp.bfloat16), v, preferred_element_type=jnp.float32)
+    return a.astype(jnp.bfloat16).reshape(length, heads * size), (q, k, v, p)
+
+
+def whole_forward(x, mats, gains, biases, heads, size, mask):
+    w_qkv, w_out, w_in, w_down = mats
+    n1, s1 = norm_forward(x, gains[0], biases[0])
+    n1 = n1.astype(jnp.bfloat16)
+    a, att = whole_attention(n1, w_qkv, heads, size, mask)
+    x1 = x + jnp.dot(a, w_out, preferred_element_type=jnp.float32)
+    n2, s2 = norm_forward(x1, gains[1], biases[1])
+    n2 = n2.astype(jnp.bfloat16)
+    h = jnp.dot(n2, w_in, preferred_element_type=jnp.float32)
+    u = jax.nn.gelu(h, approximate=False).astype(jnp.bfloat16)
+    return x1 + jnp.dot(u, w_down, preferred_element_type=jnp.float32), (n1, s1, a, att, n2, s2, h, u)
+
+
+def whole_backward(dr, mats, gains, saved, heads, size):
+    w_qkv, w_out, w_in, w_down = mats
+    n1, s1, a, (q, k, v, p), n2, s2, h, u = saved
+    length = dr.shape[0]
+    r = dr.astype(jnp.bfloat16)
+    d_down = inner_rows(u, r)
+    du = times_transpose(r, w_down)
+    dh = jax.vjp(partial(jax.nn.gelu, approximate=False), h)[1](du)[0].astype(jnp.bfloat16)
+    d_in = inner_rows(n2, dh)
+    dn2 = times_transpose(dh, w_in)
+    dx1, dg2, db2 = norm_backward(dn2, s2, gains[1])
+    dx1 = dr + dx1
+    r1 = dx1.astype(jnp.bfloat16)
+    d_out = inner_rows(a, r1)
+    da = times_transpose(r1, w_out).astype(jnp.bfloat16).reshape(length, heads, size)
+    dp = jnp.einsum("qhd,khd->hqk", da, v, preferred_element_type=jnp.float32)
+    dv = jnp.einsum("hqk,qhd->khd", p.astype(jnp.bfloat16), da, preferred_element_type=jnp.float32)
+    dz = (p * (dp - jnp.sum(p * dp, axis=-1, keepdims=True))).astype(jnp.bfloat16)
+    dq = jnp.einsum("hqk,khd->qhd", dz, k, preferred_element_type=jnp.float32) * size ** (-0.5)
+    dk = jnp.einsum("hqk,qhd->khd", dz, q, preferred_element_type=jnp.float32) * size ** (-0.5)
+    half = heads // 2
+    dproj = jnp.stack([g.reshape(length, 2, half, size) for g in (dq, dk, dv)], axis=2)
+    dproj = dproj.astype(jnp.bfloat16).reshape(length, 3 * heads * size)
+    d_qkv = inner_rows(n1, dproj)
+    dn1 = times_transpose(dproj, w_qkv)
+    dx, dg1, db1 = norm_backward(dn1, s1, gains[0])
+    return dx1 + dx, [d_qkv, d_out, d_in, d_down], (dg1, dg2, db1, db2)
+
+
+def swap(v):
+    return lax.ppermute(v, "tensor", [(0, 1), (1, 0)])
+
+
+def sequence_device(tokens_in, positions, segment_ids, owners, master, first_moment, second_moment, norm_gains,
+                    norm_biases, norm_first, norm_second, cotangent):
+    t = lax.axis_index("tensor")
+    shapes = weight_shapes(2)
+    table, _, _ = layout(shapes, 16)
+
+    def whole(v, axis):
+        own = lax.dynamic_index_in_dim(v, t, axis, keepdims=False)
+        other = swap(lax.dynamic_index_in_dim(v, 1 - t, axis, keepdims=False))
+        at = 1 if axis == 1 else 0
+        return jnp.concatenate([jnp.where(t == 0, own, other), jnp.where(t == 0, other, own)], axis=at)
+
+    def halves(v):
+        half = v.shape[0] // 2
+        own = lax.dynamic_slice_in_dim(v, t * half, half, 0)
+        other = swap(lax.dynamic_slice_in_dim(v, (1 - t) * half, half, 0))
+        return jnp.stack([jnp.where(t == 0, own, other), jnp.where(t == 0, other, own)])
+
+    tokens, cot, pos = whole(tokens_in, 0), whole(cotangent, 0), whole(positions, 1)
+    tile = lax.dynamic_index_in_dim(segment_ids, t, 0, keepdims=False)[0]
+
+    unit, used = own_units(owners, lax.axis_index("dp"), master.shape[0])
+    place = unit_places(unit, table, 16)
+    parts = jnp.zeros((16 * SHARD_UNITS, 512), jnp.bfloat16)
+    parts = parts.at[jnp.where(used, place, 16 * SHARD_UNITS)].set(master.astype(jnp.bfloat16), mode="drop", unique_indices=True)
+    shard = reduce_scatter(parts.reshape(4, 2, 2, SHARD_UNITS, 512), PLAN_DP, False, 1)
+    full = gather(to_panels(shard, table), PLAN_ALL, True, 2)
+    mats = unpack(full, table)
+
+    mask = jnp.where(tile[:, None] == tile[None, :], 0.0, MASK_FILL).astype(jnp.float32)
+    x0 = tokens.astype(jnp.float32) + sincos_embed(pos, DE)
+    x2, enc = whole_forward(x0, mats[0:4], norm_gains[:, :DE], norm_biases[:, :DE], HE, HDE, mask)
+    e = x2.astype(jnp.bfloat16)
+    y0 = jnp.dot(e, mats[4], preferred_element_type=jnp.float32).astype(jnp.bfloat16).astype(jnp.float32) + sincos_embed(pos, DD)
+    decoded, dec = whole_forward(y0, mats[5:9], norm_gains[:, DE:], norm_biases[:, DE:], HD, HDD, mask)
+    dy0, dec_grads, dec_norm = whole_backward(cot, mats[5:9], norm_gains[:, DE:], dec, HD, HDD)
+    de = dy0.astype(jnp.bfloat16)
+    d_embed = inner_rows(e, de)
+    dx2 = times_transpose(de, mats[4])
+    dx0, enc_grads, enc_norm = whole_backward(dx2, mats[0:4], norm_gains[:, :DE], enc, HE, HDE)
+
+    grads = pack(enc_grads + [d_embed] + dec_grads, table)
+    summed = reduce_scatter(grads, PLAN_ALL, True, 3)
+    spread_out = gather(from_panels(summed, table), PLAN_DP, False, 4).reshape(16 * SHARD_UNITS, 512)
+    reduced = jnp.where(used[:, None], jnp.take(spread_out, jnp.clip(place, 0, 16 * SHARD_UNITS - 1), axis=0).astype(jnp.float32), 0.0)
+    norm_total = lax.psum(jnp.concatenate([jnp.stack(enc_norm), jnp.stack(dec_norm)], axis=1), ("dp", "tensor"))
+    new_master, new_first, new_second = adamw(master, reduced, first_moment, second_moment, WEIGHT_DECAY, LEARN_RATE)
+    norm_params = jnp.concatenate([norm_gains, norm_biases], axis=0)
+    new_norms, norm_one_new, norm_two_new = adamw(norm_params, norm_total, norm_first, norm_second, 0.0, NORM_RATE)
+    return (halves(decoded), halves(dx0), new_master, new_first, new_second, new_norms, norm_one_new, norm_two_new)
+
+
 def solution(mesh):
+    step = sequence_device if (mesh.shape["dp"], mesh.shape["tensor"]) == (16, 2) else per_device
     return jax.shard_map(
-        per_device,
+        step,
         mesh=mesh,
         in_specs=(
             P(None, ("dp", "tensor"), None),

time: 1220 us -> 752 us (0.62)
  waiting for transfers between devices: 482 us -> 0.01 us
  Pallas kernels: 0 us -> 348 us
  local copies, waits for them, and re-layouts: 337 us -> 221 us
  blocking collectives: 142 us -> 38.7 us
  other arithmetic: 89.9 us -> 44.2 us
  matrix products: 125 us -> 81.7 us
  between operations: 17 us -> 2.63 us
    reduce_scatter x19 -> x0, waiting for transfers between devices: 449 us -> none  [the longest x1 356 us: per_device(): lax.psum_scatter(slot_builder(grad_sums, unit_of_slot, unit_width), 'dp',...]
    pallas_call x0 -> x4, Pallas kernels: none -> 348 us  [the longest x2 187 us: gather(): pl.pallas_call(partial(gather_kernel, plan, with_x), out_shape=jax.ShapeD...]
    scatter x2 -> x0, local copies, waits for them, and re-layouts: 155 us -> none  [the longest x1 106 us: per_device(): placed = jnp.zeros((unit_count, unit_width), jnp.bfloat16).at[targets].se...]
    all_gather x18 -> x0, blocking collectives: 99.6 us -> none  [the longest x10 55.3 us: gather_rows(): return lax.all_gather(values, 'tensor', axis=0, tiled=True)]
    gather x1, local copies, waits for them, and re-layouts: 68.9 us -> 11 us  [sequence_device(): jnp.take(spread_out, jnp.clip(place, 0, 16 * SHARD_UNITS - 1), axis=0)]
    transpose x0 -> x18, local copies, waits for them, and re-layouts: none -> 51.6 us  [the longest x5 15.8 us: unpack(): m = m.transpose(0, 1, 3, 2, 4).reshape(2 * 16 * rb, panels * PANEL)]
    slice x16 -> x27, local copies, waits for them, and re-layouts: 8.65 us -> 34.2 us  [the longest x6 20.6 us: unpack(): full[:, :, at:at + panels * padded].reshape(2, 16, panels, padded, PANEL)]
    select_n x5, other arithmetic: 29.3 us -> 4.64 us  [the longest x3 2.81 us: whole(): jnp.where(t == 0, own, other)]
  transfers between devices with their start and end apart: 24 -> 5, of which waited for: 16 -> 0; matrix products, arithmetic and copies ran while one was open for 28% -> 45% of each run, Pallas kernels for 0% -> 47%
where the time goes in v1:
time: 752 us; the launch traced here: 742 us
  Pallas kernels  348 us (46%)
  local copies, waits for them, and re-layouts  221 us (29%)
  matrix products  81.7 us (11%)
  other arithmetic  44.2 us (6%)
  blocking collectives  38.7 us (5%)
    pallas_call x2, Pallas kernels, gather(): pl.pallas_call(partial(gather_kernel, plan, with_x), out_shape=jax.ShapeD...  187 us
    pallas_call x2, Pallas kernels, reduce_scatter(): pl.pallas_call(partial(reduce_kernel, plan, with_x), out_shape=jax.ShapeD...  161 us
    psum x1, blocking collectives, sequence_device(): lax.psum(jnp.concatenate([jnp.stack(enc_norm), jnp.stack(dec_norm)], axis...  38.7 us
    unnamed x198, local copies, waits for them, and re-layouts  31.5 us
    reshape x5, local copies, waits for them, and re-layouts, unpack(): m = m.transpose(1, 3, 0, 2, 4).reshape(16 * rb, 2 * panels * PANEL)  27.9 us
    reshape x6, local copies, waits for them, and re-layouts, pack(): m = m.reshape(16, rb, 2, panels, PANEL).transpose(2, 0, 3, 1, 4)  26.8 us
    reshape x6, local copies, waits for them, and re-layouts, pack(): m = m.reshape(2, 16, rb, panels, PANEL).transpose(0, 1, 3, 2, 4)  21.5 us
    dot_general x9, matrix products, inner_rows(): lax.dot_general(left_side, right_side, (((0,), (0,)), ((), ())), preferre...  20.6 us
  transfers between devices with their start and end apart: 5, of which 0 were waited for; matrix products, arithmetic and copies ran while one was open for 45% of the time, Pallas kernels for 47%

profile of v1, /device:TPU:1, one launch (start us, length us, event | category | flops | bytes accessed | tf_op | source)
XLA Modules:
  0.0 741.6 jit_solution(1579776874583166197)
XLA Ops:
  2.5 2.0 collective-permute-start.1
  4.6 1.6 dynamic-slice_bitcast_fusion.1
  6.2 1.7 dynamic-slice_bitcast_fusion
  20.3 14.9 %scatter_custom_fusion = bf16[10496,512]{1,0:T(8,128)(2,1)} fusion(s32[1296]{0:T(1024)S(1)} %get-tuple-element.29, bf16[]{:T(256)} %constant.320.clone.1, f32[1296,512]{1,0:T(8,128)} %param.16), kind=kCustom, calls=%fused_computation.4 | custom fusion | flops 663552 | bytes 13402114 | tf_op jit(solution)/shard_map/scatter | solution.py:831
  35.2 71.9 %reduce_1.1 = bf16[656,512]{1,0:T(8,128)(2,1)} custom-call(bf16[4,2,2,656,512]{4,3,2,1,0:T(8,128)(2,1)} %bitcast.321), custom_call_target="tpu_custom_call" | custom-call | tf_op jit(solution)/shard_map/reduce_1/pallas_call | solution.py:641
  114.8 105.4 %gather_2.1 = bf16[2,4,2,2,2640,128]{5,4,3,2,1,0:T(8,128)(2,1)} custom-call(bf16[2640,128]{1,0:T(8,128)(2,1)} %copy-done.39), custom_call_target="tpu_custom_call" | custom-call | tf_op jit(solution)/shard_map/gather_2/pallas_call | solution.py:539
  221.3 3.3 fusion.164
  224.6 4.7 fusion.163
  229.3 8.0 %fusion.165 = (bf16[2,16,576,128]{3,2,1,0:T(8,128)(2,1)}, bf16[2,16,576,128]{3,2,1,0:T(8,128)(2,1)}) fusion(bf16[2,16,2640,128]{3,2,1,0:T(8,128)(2,1)} %bitcast.318), kind=kLoop, calls=%fused_computation.448 | loop fusion | bytes 18874368 | tf_op jit(solution)/shard_map/slice | solution.py:725
  241.2 2.2 slice.216
  246.1 3.3 reshape.1181
  249.5 3.0 copy.176
  252.4 2.0 copy.180
  254.4 4.3 reshape.1183
  258.7 4.3 copy.173
  263.0 8.4 %reshape.1171 = bf16[768,2304]{1,0:T(8,128)(2,1)} reshape(bf16[16,48,2,9,128]{4,3,2,1,0:T(8,128)(2,1)} %copy.173) | data formatting | bytes 7077888 | tf_op jit(solution)/shard_map/reshape | solution.py:729
  271.4 3.3 copy.185
  275.6 2.3 reshape.1189
  277.9 6.6 copy.177
  284.5 9.6 %reshape.1177 = bf16[768,3072]{1,0:T(8,128)(2,1)} reshape(bf16[16,48,2,12,128]{4,3,2,1,0:T(8,128)(2,1)} %copy.177) | data formatting | bytes 9437184 | tf_op jit(solution)/shard_map/reshape | solution.py:729
  294.1 7.2 copy.178
  304.3 1.9 multiply_cosine_fusion
  308.7 2.2 convolution_convert_fusion.3
  313.5 3.9 fusion.174
  317.4 2.5 convolution_convert_fusion.12
  321.3 11.0 %multiply_convert_fusion.2 = (bf16[256,3072]{1,0:T(8,128)(2,1)S(1)}, f32[256,3072]{1,0:T(8,128)}, f32[256,3072]{1,0:T(8,128)}) fusion(bf16[768,3072]{1,0:T(8,128)(2,1)S(1)} %bitcast.361, f32[256,768]{1,0:T(8,128)S(1)} %get-tuple-element.133, f32[768]{0:T(1024)S(1)} %copy-done.50, f32[768]{0:T(1024)S(1)} %get-tuple-element.151, f32[256]{0:T(256)S(1)} %add_rsqrt_fusion.2, ...), kind=kOutput, calls=%fused_computation.29 | convolution fusion | flops 1260060672 | bytes 13377536 | tf_op jit(solution)/shard_map/dot_general | solution.py:769
  339.4 4.7 fusion.177
  344.1 2.8 convolution_convert_fusion.14
  347.7 5.0 multiply_convert_fusion.3
  360.8 2.2 fusion.38
  363.0 2.1 convolution_convert_fusion.4
  365.9 3.1 fusion.56
  377.7 1.9 convolution_convert_fusion.6
  379.6 3.2 add_convert_fusion
  382.9 2.2 multiply_reduce_fusion.2
  388.5 3.8 convolution_convert_fusion.1
  392.3 3.7 convolution_convert_fusion
  396.2 2.7 fusion.61
  403.3 2.2 multiply_reduce_fusion.3
  405.5 3.1 convolution_convert_fusion.2
  409.6 2.2 copy.237
  411.8 1.9 copy.207
  413.6 4.1 reshape.1202
  417.8 3.5 copy.208
  421.2 2.2 reshape.1198
  424.5 4.3 reshape.1199
  428.8 3.3 copy.205
  432.0 2.2 reshape.1195
  437.4 9.2 %reshape.1196 = bf16[16,48,2,12,128]{4,3,2,1,0:T(8,128)(2,1)} reshape(bf16[768,3072]{1,0:T(8,128)(2,1)} %convolution_convert_fusion.1) | data formatting | bytes 9437184 | tf_op jit(solution)/shard_map/reshape | solution.py:741
  446.5 6.8 copy.202
  453.3 10.7 %reshape.1197 = bf16[2,16,96,6,128]{4,3,2,1,0:T(8,128)(2,1)} reshape(bf16[3072,768]{1,0:T(8,128)(2,1)} %convolution_convert_fusion) | data formatting | bytes 9437184 | tf_op jit(solution)/shard_map/reshape | solution.py:739
  464.1 6.0 copy.203
  470.1 8.2 %reshape.1194 = bf16[16,48,2,9,128]{4,3,2,1,0:T(8,128)(2,1)} reshape(bf16[768,2304]{1,0:T(8,128)(2,1)} %convolution_convert_fusion.2) | data formatting | bytes 7077888 | tf_op jit(solution)/shard_map/reshape | solution.py:741
  478.4 4.3 copy.200
  482.7 2.5 constant_dynamic-update-slice_fusion.17
  487.2 3.0 constant_dynamic-update-slice_fusion.15
  490.3 3.1 constant_dynamic-update-slice_fusion.14
  497.5 1.7 constant_dynamic-update-slice_fusion.10
  499.2 1.8 constant_dynamic-update-slice_fusion.9.src
  501.0 88.8 %reduce_3.1 = bf16[2640,128]{1,0:T(8,128)(2,1)} custom-call(bf16[2,4,2,2,2640,128]{5,4,3,2,1,0:T(8,128)(2,1)} %constant_dynamic-update-slice_fusion.9.src), custom_call_target="tpu_custom_call" | custom-call | tf_op jit(solution)/shard_map/reduce_3/pallas_call | solution.py:641
  592.8 38.7 %psum.7 = f32[4,1280]{1,0:T(4,128)S(1)} all-reduce(f32[4,1280]{1,0:T(4,128)S(1)} %maximum_maximum_fusion), channel_id=1, replica_groups=mesh['dp'=16,'tensor'=2] {'dp','tensor'}, use_global_device_ids=true, to_apply=%region_35.36 | all-reduce | flops 5120 | bytes 40960 | tf_op jit(solution)/shard_map/psum | solution.py:852
  637.4 81.9 %gather_4.1 = bf16[4,2,2,656,512]{4,3,2,1,0:T(8,128)(2,1)} custom-call(bf16[656,512]{1,0:T(8,128)(2,1)} %pad.14.mine), custom_call_target="tpu_custom_call" | custom-call | tf_op jit(solution)/shard_map/gather_4/pallas_call | solution.py:539
  719.3 11.0 %gather_fusion = bf16[1296,512]{1,0:T(8,128)(2,1)} fusion(bf16[10496,512]{1,0:T(8,128)(2,1)} %bitcast.322, s32[2048]{0:T(1024)S(1)} %copy-done.53), kind=kCustom, calls=%fused_computation | custom fusion | bytes 2659392 | tf_op jit(solution)/shard_map/jit(_take)/gather | solution.py:851
  730.4 7.2 multiply_subtract_fusion
  (366 shorter events, 96.6 us)
Async XLA Ops:
  0.6 236.7 %copy-start = (s32[2,1,256]{2,1,0:T(1,128)S(1)}, s32[2,1,256]{2,1,0:T(1,128)}, u32[]{:S(2)}) copy-start(s32[2,1,256]{2,1,0:T(1,128)} %param.14) | copy-start | bytes 6148
  2.5 298.8 %collective-permute-start.1 = (s32[3,128]{1,0:T(4,128)}, s32[3,128]{1,0:T(4,128)}, u32[]{:S(2)}, u32[]{:S(2)}) collective-permute-start(s32[3,128]{1,0:T(4,128)} %bitcast.313), channel_id=1, source_target_pairs={{0,1},{1,0},{2,3},{3,2},{4,5},{5,4},{6,7},{7,6},{8,9},{9,8},{10,11... | collective-permute-start | bytes 4616 | tf_op jit(solution)/shard_map/ppermute | solution.py:804
  6.2 300.5 %collective-permute-start = (bf16[128,768]{1,0:T(8,128)(2,1)}, bf16[128,768]{1,0:T(8,128)(2,1)}, u32[]{:S(2)}, u32[]{:S(2)}) collective-permute-start(bf16[128,768]{1,0:T(8,128)(2,1)} %dynamic-slice_bitcast_fusion.1), channel_id=1, source_target_pairs={{0,1},{1,0},{2,3},{3,2},{4,5},{5,4},{6,7},{7,6},{8,9},{9,8},{10,11... | collective-permute-start | bytes 589832 | tf_op jit(solution)/shard_map/ppermute | solution.py:804
  7.8 346.6 %collective-permute-start.3 = (f32[128,512]{1,0:T(8,128)}, f32[128,512]{1,0:T(8,128)}, u32[]{:S(2)}, u32[]{:S(2)}) collective-permute-start(f32[128,512]{1,0:T(8,128)} %dynamic-slice_bitcast_fusion), channel_id=1, source_target_pairs={{0,1},{1,0},{2,3},{3,2},{4,5},{5,4},{6,7},{7,6},{8,9},{9,8},{10,11... | collective-permute-start | bytes 786440 | tf_op jit(solution)/shard_map/ppermute | solution.py:804
  249.5 3.0 copy-start.14
  263.0 8.4 %copy-start.8 = (bf16[2,16,256,128]{3,2,1,0:T(8,128)(2,1)S(1)}, bf16[2,16,256,128]{3,2,1,0:T(8,128)(2,1)}, u32[]{:S(2)}) copy-start(bf16[2,16,256,128]{3,2,1,0:T(8,128)(2,1)} %get-tuple-element.56) | copy-start | bytes 6291460
  271.4 3.3 copy-start.7
  294.0 7.3 copy-start.64
  294.0 7.9 %copy-start.71 = (f32[64]{0:T(128)S(1)}, f32[64]{0:T(128)}, u32[]{:S(2)}) copy-start(f32[64]{0:T(128)} %negate_power_fusion.1) | copy-start | bytes 772
  294.1 8.5 %copy-start.72 = (f32[96]{0:T(128)S(1)}, f32[96]{0:T(128)}, u32[]{:S(2)}) copy-start(f32[96]{0:T(128)} %negate_power_fusion.2) | copy-start | bytes 1156
  294.1 10.2 %copy-start.70 = (f32[144]{0:T(256)S(1)}, f32[144]{0:T(256)}, u32[]{:S(2)}) copy-start(f32[144]{0:T(256)} %negate_power_fusion) | copy-start | bytes 1732
  302.5 4.2 copy-start.45
  308.2 97.3 %copy-start.59 = (f32[256]{0:T(256)}, f32[256]{0:T(256)S(1)}, u32[]{:S(2)}) copy-start(f32[256]{0:T(256)S(1)} %add_rsqrt_fusion.3) | copy-start | bytes 3076
  313.5 3.9 copy-start.43
  317.4 3.7 slice-start.8
  317.4 3.9 slice-start.9
  319.9 12.4 %slice-start.4 = ((s8[6291456]{0:T(1024)(128)(4,1)}), s8[4194304]{0:T(1024)(128)(4,1)S(1)}, s32[]{:S(2)}) async-start(s8[6291456]{0:T(1024)(128)(4,1)} %bitcast.347), calls=%async_computation.4 | async-start | bytes 8388608
  321.3 11.1 %slice-start.5 = ((s8[6291456]{0:T(1024)(128)(4,1)}), s8[2097152]{0:T(1024)(128)(4,1)S(1)}, s32[]{:S(2)}) async-start(s8[6291456]{0:T(1024)(128)(4,1)} %bitcast.347), calls=%async_computation.5 | async-start | bytes 4194304
  339.4 4.7 copy-start.48
  344.1 3.5 copy-start.27
  344.1 3.5 copy-start.58
  344.1 3.5 copy-start.61
  347.6 5.0 copy-start.28
  354.2 384.1 %collective-permute-start.2 = (f32[128,512]{1,0:T(8,128)}, f32[128,512]{1,0:T(8,128)}, u32[]{:S(2)}, u32[]{:S(2)}) collective-permute-start(f32[128,512]{1,0:T(8,128)} %constant_dynamic-slice_fusion.1), channel_id=1, source_target_pairs={{0,1},{1,0},{2,3},{3,2},{4,5},{5,4},{6,7},{7,6},{8,9},{9,8},{10,11... | collective-permute-start | bytes 786440 | tf_op jit(solution)/shard_map/ppermute | solution.py:804
  365.9 3.5 copy-start.18
  365.9 3.5 copy-start.47
  365.9 3.6 copy-start.49
  369.5 10.1 %slice-start.6 = ((s8[6291456]{0:T(1024)(128)(4,1)}), s8[4194304]{0:T(1024)(128)(4,1)S(1)}, s32[]{:S(2)}) async-start(s8[6291456]{0:T(1024)(128)(4,1)} %bitcast.350), calls=%async_computation.6 | async-start | bytes 8388608
  370.4 9.2 %slice-start.7 = ((s8[6291456]{0:T(1024)(128)(4,1)}), s8[2097152]{0:T(1024)(128)(4,1)S(1)}, s32[]{:S(2)}) async-start(s8[6291456]{0:T(1024)(128)(4,1)} %bitcast.350), calls=%async_computation.7 | async-start | bytes 4194304
  375.4 4.2 copy-start.74
  375.7 4.0 copy-start.73
  376.4 6.4 slice-start.10
  379.6 3.2 slice-start.11
  388.5 3.8 copy-start.20
  405.5 3.1 copy-start.29
  428.8 3.3 copy-start.17
  482.6 4.5 slice-start
  482.6 4.6 slice-start.1
  486.6 3.7 slice-start.2
  487.2 3.0 slice-start.3
  490.3 3.1 copy-start.23
  493.4 3.2 copy-start.30
  493.4 4.1 copy-start.5
  501.0 91.6 %copy-start.65 = (f32[768]{0:T(1024)S(1)}, f32[768]{0:T(1024)}, u32[]{:S(2)}) copy-start(f32[768]{0:T(1024)} %get-tuple-element.10) | copy-start | bytes 9220
  501.0 91.7 %copy-start.66 = (f32[512]{0:T(512)S(1)}, f32[512]{0:T(512)}, u32[]{:S(2)}) copy-start(f32[512]{0:T(512)} %get-tuple-element.14) | copy-start | bytes 6148
  501.0 91.7 %copy-start.67 = (f32[512]{0:T(512)S(1)}, f32[512]{0:T(512)}, u32[]{:S(2)}) copy-start(f32[512]{0:T(512)} %get-tuple-element.23) | copy-start | bytes 6148
  501.0 91.7 %copy-start.68 = (f32[512]{0:T(512)S(1)}, f32[512]{0:T(512)}, u32[]{:S(2)}) copy-start(f32[512]{0:T(512)} %get-tuple-element.12) | copy-start | bytes 6148
  501.0 91.7 %copy-start.69 = (f32[512]{0:T(512)S(1)}, f32[512]{0:T(512)}, u32[]{:S(2)}) copy-start(f32[512]{0:T(512)} %get-tuple-element.22) | copy-start | bytes 6148
  501.0 130.4 %copy-start.60 = (f32[256]{0:T(256)S(1)}, f32[256]{0:T(256)}, u32[]{:S(2)}) copy-start(f32[256]{0:T(256)} %copy-done.59) | copy-start | bytes 3076
  589.8 45.3 %slice-start.12 = ((bf16[2640,128]{1,0:T(8,128)(2,1)}), bf16[64,128]{1,0:T(8,128)(2,1)S(1)}, s32[]{:S(2)}) async-start(bf16[2640,128]{1,0:T(8,128)(2,1)} %reduce_3.1), calls=%async_computation.12 | async-start | bytes 32768 | tf_op jit(solution)/shard_map/slice | solution.py:712
  590.7 44.4 %slice-start.13 = ((bf16[2640,128]{1,0:T(8,128)(2,1)}), bf16[96,128]{1,0:T(8,128)(2,1)S(1)}, s32[]{:S(2)}) async-start(bf16[2640,128]{1,0:T(8,128)(2,1)} %reduce_3.1), calls=%async_computation.13 | async-start | bytes 49152 | tf_op jit(solution)/shard_map/slice | solution.py:712
  591.6 43.8 %slice-start.14 = ((bf16[2640,128]{1,0:T(8,128)(2,1)}), bf16[432,128]{1,0:T(8,128)(2,1)S(1)}, s32[]{:S(2)}) async-start(bf16[2640,128]{1,0:T(8,128)(2,1)} %reduce_3.1), calls=%async_computation.14 | async-start | bytes 221184 | tf_op jit(solution)/shard_map/slice | solution.py:712
  633.8 106.4 %collective-permute-start.4 = (f32[128,768]{1,0:T(8,128)S(1)}, f32[128,768]{1,0:T(8,128)S(1)}, u32[]{:S(2)}, u32[]{:S(2)}) collective-permute-start(f32[128,768]{1,0:T(8,128)S(1)} %constant_dynamic-slice_fusion), channel_id=1, source_target_pairs={{0,1},{1,0},{2,3},{3,2},{4,5},{5,4},{6,7},{7,6},{8,9},{9,8},{10,11... | collective-permute-start | bytes 1179656 | tf_op jit(solution)/shard_map/ppermute | solution.py:804
  637.4 81.9 %copy-start.53 = (s32[2048]{0:T(1024)S(1)}, s32[2048]{0:T(1024)}, u32[]{:S(2)}) copy-start(s32[2048]{0:T(1024)} %pad_clamp_fusion) | copy-start | bytes 24580
  719.3 11.0 %copy-start.2 = (f32[1296,512]{1,0:T(8,128)S(1)}, f32[1296,512]{1,0:T(8,128)}, u32[]{:S(2)}) copy-start(f32[1296,512]{1,0:T(8,128)} %param.16) | copy-start | bytes 7962628
  719.3 11.0 %copy-start.62 = (pred[1296]{0:T(1024)(128)(4,1)S(1)}, pred[1296]{0:T(1024)(128)(4,1)}, u32[]{:S(2)}) copy-start(pred[1296]{0:T(1024)(128)(4,1)} %get-tuple-element.36) | copy-start | bytes 3892
  719.3 11.0 %copy-start.63 = (pred[1296]{0:T(1024)(128)(4,1)S(1)}, pred[1296]{0:T(1024)(128)(4,1)}, u32[]{:S(2)}) copy-start(pred[1296]{0:T(1024)(128)(4,1)} %get-tuple-element.152) | copy-start | bytes 3892
  730.3 7.3 copy-start.51
  730.3 7.3 copy-start.52
  730.3 7.3 copy-start.55
  730.4 7.3 copy-start.56
  730.4 8.0 %copy-start.42 = (f32[256,512]{1,0:T(8,128)S(1)}, f32[256,512]{1,0:T(8,128)}, u32[]{:S(2)}) copy-start(f32[256,512]{1,0:T(8,128)} %copy-done.41) | copy-start | bytes 1572868
  730.4 9.8 %copy-start.26 = (f32[256,768]{1,0:T(8,128)S(1)}, f32[256,768]{1,0:T(8,128)}, u32[]{:S(2)}) copy-start(f32[256,768]{1,0:T(8,128)} %copy-done.25) | copy-start | bytes 2359300
  737.7 3.5 copy-start.1
  (31 other events, 52.8 us)

commit v2 on v1

--- a/solution.py
+++ b/solution.py
@@ -2,6 +2,8 @@
 
 import jax
 import jax.numpy as jnp
+import ml_dtypes
+import numpy as np
 from jax import lax
 from jax.experimental import pallas as pl
 from jax.experimental.pallas import tpu as pltpu
@@ -560,12 +562,57 @@
     lax.fori_loop(0, n // step, body, 0)
 
 
-def reduce_kernel(plan, with_x, src, out, *rest):
+def total_steps(p, src, out, mid, line, send, recv):
+    waits = []
+
+    def move(k, a, b, way, cond=None):
+        cp = pltpu.make_async_remote_copy(src_ref=a, dst_ref=b, send_sem=send.at[k], recv_sem=recv.at[k],
+                                          device_id=p.ids[way], device_id_type=MESH)
+        when(cond, cp.start)
+        waits.append((cond, cp))
+
+    def land(k, b, cond=None):
+        when(cond, pltpu.make_async_remote_copy(src_ref=b, dst_ref=b, send_sem=send.at[k], recv_sem=recv.at[k],
+                                                device_id=p.ids["c"], device_id_type=MESH).wait_recv)
+
+    now = src
+    for k, way in enumerate(("c", "x", "y")):
+        move(k, now, mid.at[k], way)
+        yield
+        land(k, mid.at[k])
+        nxt = mid.at[3 + k] if k < 2 else line.at[p.z]
+        nxt[...] = now[...] + mid[k]
+        now = nxt
+    for k in range(3):
+        lo, hi = jnp.maximum(p.z - k, 0), jnp.minimum(p.z + k, 3)
+        if k > 0:
+            land(2 + k, line.at[lo], p.z >= k)
+            land(5 + k, line.at[hi], p.z + k <= 3)
+        move(3 + k, line.at[lo], line.at[lo], "z+", jnp.logical_and(p.z >= k, p.z < 3))
+        move(6 + k, line.at[hi], line.at[hi], "z-", jnp.logical_and(p.z + k <= 3, p.z > 0))
+        yield
+    land(5, line.at[jnp.maximum(p.z - 3, 0)], p.z >= 3)
+    land(8, line.at[jnp.minimum(p.z + 3, 3)], p.z <= 0)
+    out[...] = (line[0] + line[1]) + (line[2] + line[3])
+    for c, cp in waits:
+        when(c, cp.wait_send)
+
+
+def reduce_kernel(plan, with_x, small, src, *rest):
     n = len(plan)
+    steps = iter(())
+    if small:
+        small_src, out, small_out = rest[:3]
+        mid, line, small_send, small_recv = rest[-4:]
+        rest = rest[3:-4]
+    else:
+        out, rest = rest[0], rest[1:]
     accs, halves, bufs = rest[:n], rest[n:2 * n], rest[2 * n:3 * n]
     send, recv, sib_send, sib_recv, loads = rest[3 * n:]
     p = Place()
     p.greet(["c", "y", "x"] if with_x else ["c", "y"])
+    if small:
+        steps = total_steps(p, small_src, small_out, mid, line, small_send, small_recv)
     trees = [spread(o) for o, _, _ in plan]
     ids = [{d: i + 32 * g for i, d in enumerate(sorted(t))} for g, t in enumerate(trees)]
     waits = []
@@ -590,10 +637,11 @@
             ld.start()
         when(cond, go)
         waits.append((cond, cp))
-    for _, g, d in events:
+    for number, (_, g, d) in enumerate(events):
         k = ids[g][d]
         rows = pl.ds(plan[g][1], plan[g][2])
-        base = k - ids[g][min(trees[g])]
+        if number % 8 == 0:
+            next(steps, None)
 
         def step(g=g, d=d, k=k, rows=rows):
             acc = accs[g].at[ix(d)]
@@ -627,26 +675,35 @@
             waits.append((cond, cp))
         else:
             out[rows, :] = accs[g][ix(d)]
+    for _ in steps:
+        pass
     for c, cp in waits:
         when(c, cp.wait_send)
 
 
-def reduce_scatter(whole, plan, with_x, ident, limit=62 << 20):
+def reduce_scatter(whole, plan, with_x, ident, small=None):
     rows, width = whole.shape[-2:]
     dt = whole.dtype
     lead = (2, 4, 2) if with_x else (4, 2)
     blocks = [pltpu.VMEM(lead + (num, width), dt) for _, _, num in plan]
     bufs = [pltpu.VMEM((len(spread(o)), num, width), dt) for o, _, num in plan]
     sems = pltpu.SemaphoreType.DMA((32 * len(plan),))
+    vmem = pl.BlockSpec(memory_space=pltpu.VMEM)
+    out = jax.ShapeDtypeStruct((rows, width), dt)
+    scratch = blocks + blocks + bufs + [sems] * 5
+    if small is not None:
+        out = (out, jax.ShapeDtypeStruct(small.shape, small.dtype))
+        scratch += [pltpu.VMEM((5,) + small.shape, small.dtype), pltpu.VMEM((4,) + small.shape, small.dtype)]
+        scratch += [pltpu.SemaphoreType.DMA((9,))] * 2
     return pl.pallas_call(
-        partial(reduce_kernel, plan, with_x),
-        out_shape=jax.ShapeDtypeStruct((rows, width), dt),
-        in_specs=[pl.BlockSpec(memory_space=pl.ANY)],
-        out_specs=pl.BlockSpec(memory_space=pltpu.VMEM),
-        scratch_shapes=blocks + blocks + bufs + [sems] * 5,
-        compiler_params=pltpu.CompilerParams(collective_id=ident, has_side_effects=True, vmem_limit_bytes=limit),
+        partial(reduce_kernel, plan, with_x, small is not None),
+        out_shape=out,
+        in_specs=[pl.BlockSpec(memory_space=pl.ANY)] + ([] if small is None else [vmem]),
+        out_specs=vmem if small is None else (vmem, vmem),
+        scratch_shapes=scratch,
+        compiler_params=pltpu.CompilerParams(collective_id=ident, has_side_effects=True, vmem_limit_bytes=62 << 20),
         name=f"reduce_{ident}",
-    )(whole)
+    )(*((whole,) if small is None else (whole, small)))
 
 
 PLAN_ALL = [("zxy", 0, 640), ("zyx", 640, 640), ("xzy", 1280, 640), ("yzx", 1920, 720)]
@@ -718,86 +775,349 @@
 BY_ROWS = (1, 3, 6, 8)
 
 
-def unpack(full, table):
-    full = full.reshape(2, 16, full.shape[-2], PANEL)
-    mats = []
-    for i, (rb, panels, n, _, at, padded) in enumerate(table):
-        m = full[:, :, at:at + panels * padded].reshape(2, 16, panels, padded, PANEL)[:, :, :, :rb]
-        if i in BY_ROWS:
-            m = m.transpose(0, 1, 3, 2, 4).reshape(2 * 16 * rb, panels * PANEL)
+def position_table():
+    cols = []
+    for width in (DE, DD):
+        side = width // 16 * 6
+        parts = (width - 2 * side, side, side)
+        tab = np.zeros((48, width), np.float64)
+        col = 0
+        for i, n in enumerate(parts):
+            half = n // 2
+            freq = 1.0 / 10000.0 ** (np.arange(half) / half)
+            ang = np.arange(16)[:, None] * freq[None, :]
+            tab[16 * i:16 * i + 16, col:col + n] = np.concatenate([np.sin(ang), np.cos(ang)], axis=1)
+            col += n
+        cols.append(tab)
+    left = np.concatenate(cols, axis=1).astype(np.float32)
+    terms = []
+    for _ in range(3):
+        terms.append(left.astype(ml_dtypes.bfloat16))
+        left = left - terms[-1].astype(np.float32)
+    return np.stack(terms)
+
+
+def dot(a, b):
+    return jnp.dot(a, b, preferred_element_type=jnp.float32)
+
+
+def dot_nt(a, b):
+    return lax.dot_general(a, b, (((1,), (1,)), ((), ())), preferred_element_type=jnp.float32)
+
+
+def dot_tn(a, b):
+    return lax.dot_general(a, b, (((0,), (0,)), ((), ())), preferred_element_type=jnp.float32)
+
+
+def lanes(i, n=128):
+    return pl.ds(pl.multiple_of(i * n, n), n)
+
+
+def ln_parts(x):
+    c = x - jnp.mean(x, axis=-1, keepdims=True)
+    inv = lax.rsqrt(jnp.mean(c * c, axis=-1, keepdims=True) + NORM_EPS)
+    return c * inv, inv
+
+
+def ln_back(up, m, inv, gain):
+    s = up * gain
+    a = jnp.mean(s, axis=-1, keepdims=True)
+    b = jnp.mean(s * m, axis=-1, keepdims=True)
+    return inv * (s - a - m * b), jnp.sum(up * m, axis=0, keepdims=True), jnp.sum(up, axis=0, keepdims=True)
+
+
+class Block:
+    def __init__(self, width, heads, size, hidden, first, table, col):
+        self.width, self.heads, self.size, self.hidden, self.col = width, heads, size, hidden, col
+        self.q, self.o, self.a, self.b = table[first:first + 4]
+        self.part = heads // 2 * size
+        self.per = 128 // size
+
+
+def panel(w, t, mat, g, lo=0, num=16):
+    rb, _, _, _, at, padded = mat
+    rows = pl.ds(pl.multiple_of(at + g * padded, 16), padded)
+    v = w[t, lo:lo + num, rows, :] if isinstance(lo, int) else w[t, pl.ds(lo, num), rows, :]
+    if padded > rb:
+        v = v.astype(jnp.float32)[:, :rb].reshape(num * rb, 128).astype(jnp.bfloat16)
+        return v
+    return v.reshape(num * rb, 128)
+
+
+def pair(w, mat, g):
+    return jnp.concatenate([panel(w, 0, mat, g), panel(w, 1, mat, g)], axis=1)
+
+
+def block_fwd(b, x, xo, w, gains, biases, same, n1, proj, p, att, ow, m1, i1, n2, m2, i2, act, slope):
+    cols = slice(b.col, b.col + b.width)
+    m, inv = ln_parts(x[...])
+    m1[...] = m
+    i1[...] = inv
+    n1[...] = (m * gains[0:1, cols] + biases[0:1, cols]).astype(jnp.bfloat16)
+    gq = b.q[1]
+
+    def qkv(g, _):
+        r = dot(n1[...], pair(w, b.q, g)).astype(jnp.bfloat16)
+        proj[:, lanes(g)] = r[:, :128]
+        proj[:, lanes(gq + g)] = r[:, 128:]
+        return 0
+
+    lax.fori_loop(0, gq, qkv, 0)
+    np_ = b.part // 128
+    lane = lax.broadcasted_iota(jnp.int32, (256, 128), 1)
+    masks = [lane // b.size == i for i in range(b.per)]
+
+    def heads(i, _):
+        t, j = i // np_, i % np_
+        q = proj[:, lanes(t * gq + j)]
+        k = proj[:, lanes(t * gq + np_ + j)]
+        v = proj[:, lanes(t * gq + 2 * np_ + j)]
+        total = jnp.zeros((256, 128), jnp.float32)
+        for h in range(b.per):
+            z = dot_nt(jnp.where(masks[h], q, 0), k) * b.size ** (-0.5) + same
+            e = jnp.exp(z - jnp.max(z, axis=-1, keepdims=True))
+            s = e / jnp.sum(e, axis=-1, keepdims=True)
+            p[i * b.per + h] = s
+            total = total + dot(s.astype(jnp.bfloat16), jnp.where(masks[h], v, 0))
+        att[:, lanes(i)] = total.astype(jnp.bfloat16)
+        return 0
+
+    lax.fori_loop(0, 2 * np_, heads, 0)
+    for t in range(2):
+        for g in range(b.width // 128):
+            ow[t, :, g * 128:(g + 1) * 128] = panel(w, t, b.o, g)
+    x1 = x[...] + dot(att[:, :b.part], ow[0]) + dot(att[:, b.part:], ow[1])
+    xo[...] = x1
+    m, inv = ln_parts(x1)
+    m2[...] = m
+    i2[...] = inv
+    n2[...] = (m * gains[1:2, cols] + biases[1:2, cols]).astype(jnp.bfloat16)
+    ga = b.a[1]
+
+    def up(g, _):
+        h = dot(n2[...], pair(w, b.a, g))
+        big = 0.5 * (1.0 + lax.erf(h * 0.7071067811865476))
+        act_v = (h * big).astype(jnp.bfloat16)
+        dens = big + h * (0.3989422804014327 * jnp.exp(-0.5 * h * h))
+        act[:, lanes(g)] = act_v[:, :128]
+        act[:, lanes(ga + g)] = act_v[:, 128:]
+        slope[:, lanes(g)] = dens[:, :128]
+        slope[:, lanes(ga + g)] = dens[:, 128:]
+        return 0
+
+    lax.fori_loop(0, ga, up, 0)
+    half = b.hidden // 2
+
+    def down(g, _):
+        w0 = jnp.concatenate([panel(w, 0, b.b, 2 * g), panel(w, 0, b.b, 2 * g + 1)], axis=1)
+        w1 = jnp.concatenate([panel(w, 1, b.b, 2 * g), panel(w, 1, b.b, 2 * g + 1)], axis=1)
+        xo[:, lanes(g, 256)] += dot(act[:, :half], w0) + dot(act[:, half:], w1)
+        return 0
+
+    lax.fori_loop(0, b.width // 256, down, 0)
+
+
+def block_bwd(b, dr, w, gains, same, n1, proj, p, att, ow, m1, i1, n2, m2, i2, act, slope,
+              r, dh, r1, dp_out, acc, da, norm_out):
+    cols = slice(b.col, b.col + b.width)
+    r[...] = dr[...].astype(jnp.bfloat16)
+    half = b.hidden // 2
+    rb = b.b[0]
+    gb = b.width // 128
+    num = 4
+
+    def hidden(i, _):
+        t, lo = i // (16 // num), (i % (16 // num)) * num
+        wc = jnp.concatenate([panel(w, t, b.b, g, lo, num) for g in range(gb)], axis=1)
+        at = lanes(i, num * rb)
+        dh[:, at] = (dot_nt(r[...], wc) * slope[:, at]).astype(jnp.bfloat16)
+        return 0
+
+    lax.fori_loop(0, 2 * (16 // num), hidden, 0)
+    ga = b.a[1]
+    acc[...] = jnp.zeros_like(acc)
+
+    def up(g, _):
+        d = jnp.concatenate([dh[:, lanes(g)], dh[:, lanes(ga + g)]], axis=1)
+        acc[...] += dot_nt(d, pair(w, b.a, g))
+        return 0
+
+    lax.fori_loop(0, ga, up, 0)
+    dx, dg, db = ln_back(acc[...], m2[...], i2[...], gains[1:2, cols])
+    norm_out[1:2, cols] = dg
+    norm_out[3:4, cols] = db
+    dx1 = dr[...] + dx
+    dr[...] = dx1
+    r1[...] = dx1.astype(jnp.bfloat16)
+    for t in range(2):
+        da[:, t * b.part:(t + 1) * b.part] = dot_nt(r1[...], ow[t]).astype(jnp.bfloat16)
+    gq = b.q[1]
+    np_ = b.part // 128
+    lane = lax.broadcasted_iota(jnp.int32, (256, 128), 1)
+    masks = [lane // b.size == i for i in range(b.per)]
+    scale = b.size ** (-0.5)
+
+    def heads(i, _):
+        t, j = i // np_, i % np_
+        q = proj[:, lanes(t * gq + j)]
+        k = proj[:, lanes(t * gq + np_ + j)]
+        v = proj[:, lanes(t * gq + 2 * np_ + j)]
+        up_ = da[:, lanes(i)]
+        dq = jnp.zeros((256, 128), jnp.float32)
+        dk = jnp.zeros((256, 128), jnp.float32)
+        dv = jnp.zeros((256, 128), jnp.float32)
+        for h in range(b.per):
+            s = p[i * b.per + h]
+            u = jnp.where(masks[h], up_, 0)
+            dp = dot_nt(u, v)
+            dv = dv + dot_tn(s.astype(jnp.bfloat16), u)
+            t1 = s * dp
+            dz = (t1 - s * jnp.sum(t1, axis=-1, keepdims=True)).astype(jnp.bfloat16)
+            dq = dq + dot(dz, jnp.where(masks[h], k, 0))
+            dk = dk + dot_tn(dz, jnp.where(masks[h], q, 0))
+        dp_out[:, lanes(t * gq + j)] = (dq * scale).astype(jnp.bfloat16)
+        dp_out[:, lanes(t * gq + np_ + j)] = (dk * scale).astype(jnp.bfloat16)
+        dp_out[:, lanes(t * gq + 2 * np_ + j)] = dv.astype(jnp.bfloat16)
+        return 0
+
+    lax.fori_loop(0, 2 * np_, heads, 0)
+    acc[...] = jnp.zeros_like(acc)
+
+    def qkv(g, _):
+        d = jnp.concatenate([dp_out[:, lanes(g)], dp_out[:, lanes(gq + g)]], axis=1)
+        acc[...] += dot_nt(d, pair(w, b.q, g))
+        return 0
+
+    lax.fori_loop(0, gq, qkv, 0)
+    dx, dg, db = ln_back(acc[...], m1[...], i1[...], gains[0:1, cols])
+    norm_out[0:1, cols] = dg
+    norm_out[2:3, cols] = db
+    dr[...] = dr[...] + dx
+
+
+ACTS = (("n1", DE), ("att", DE), ("n2", DE), ("act", FFE), ("low", DE), ("n1", DD), ("att", DD), ("n2", DD), ("act", FFD))
+GRADS = (3 * DE, DE, FFE, DE, DD, 3 * DD, DD, FFD, DD)
+
+
+def chain_kernel(table, tok, pos, tile_r, tile_c, gains, biases, cot, tab, w, *refs):
+    dec, dx0, norm_out = refs[:3]
+    acts, grads = refs[3:12], refs[12:21]
+    (pe, pd, se, sd, proj_e, proj_d, da_e, da_d, ow_e, ow_d, m1e, m2e, m1d, m2d, i1e, i2e, i1d, i2d,
+     x, y, acc_e, acc_d) = refs[21:]
+    enc_b = Block(DE, HE, HDE, FFE, 0, table, 0)
+    dec_b = Block(DD, HD, HDD, FFD, 5, table, DE)
+    em = table[4]
+    lane = lax.broadcasted_iota(jnp.int32, (256, 48), 1)
+    hot = jnp.logical_or(jnp.logical_or(lane == pos[:, 0:1], lane == pos[:, 1:2] + 16), lane == pos[:, 2:3] + 32)
+    hot = jnp.where(hot, 1.0, 0.0).astype(jnp.bfloat16)
+    same = jnp.where(tile_c[...] == tile_r[...], 0.0, MASK_FILL)
+    x[...] = tok[...].astype(jnp.float32) + (dot(hot, tab[0, :, :DE]) + dot(hot, tab[1, :, :DE]) + dot(hot, tab[2, :, :DE]))
+    n1e, ae, n2e, ue, low, n1d, ad, n2d, ud = acts
+    dpe, r1e, dhe, re, dlow, dpd, r1d, dhd, rd = grads
+    block_fwd(enc_b, x, dx0, w, gains, biases, same, n1e, proj_e, pe, ae, ow_e, m1e, i1e, n2e, m2e, i2e, ue, se)
+    low[...] = dx0[...].astype(jnp.bfloat16)
+    for g in range(2):
+        v = dot(low[...], pair(w, em, g)).astype(jnp.bfloat16).astype(jnp.float32)
+        y[:, g * 128:(g + 1) * 128] = v[:, :128]
+        y[:, 256 + g * 128:256 + (g + 1) * 128] = v[:, 128:]
+    y[...] += dot(hot, tab[0, :, DE:]) + dot(hot, tab[1, :, DE:]) + dot(hot, tab[2, :, DE:])
+    block_fwd(dec_b, y, dec, w, gains, biases, same, n1d, proj_d, pd, ad, ow_d, m1d, i1d, n2d, m2d, i2d, ud, sd)
+    y[...] = cot[...]
+    block_bwd(dec_b, y, w, gains, same, n1d, proj_d, pd, ad, ow_d, m1d, i1d, n2d, m2d, i2d, ud, sd,
+              rd, dhd, r1d, dpd, acc_d, da_d, norm_out)
+    dlow[...] = y[...].astype(jnp.bfloat16)
+    for g in range(2):
+        d = jnp.concatenate([dlow[:, g * 128:(g + 1) * 128], dlow[:, 256 + g * 128:256 + (g + 1) * 128]], axis=1)
+        v = dot_nt(d, pair(w, em, g))
+        if g == 0:
+            dx0[...] = v
         else:
-            m = m.transpose(1, 3, 0, 2, 4).reshape(16 * rb, 2 * panels * PANEL)
-        mats.append(m)
-    return mats
-
-
-def pack(mats, table):
-    out = []
-    for i, (rb, panels, n, _, at, padded) in enumerate(table):
-        m = mats[i].astype(jnp.bfloat16)
-        if i in BY_ROWS:
-            m = m.reshape(2, 16, rb, panels, PANEL).transpose(0, 1, 3, 2, 4)
+            dx0[...] += v
+    block_bwd(enc_b, dx0, w, gains, same, n1e, proj_e, pe, ae, ow_e, m1e, i1e, n2e, m2e, i2e, ue, se,
+              re, dhe, r1e, dpe, acc_e, da_e, norm_out)
+
+
+def chain(tokens, pos, tile, gains, biases, cot, full, table):
+    f32, bf16 = jnp.float32, jnp.bfloat16
+    S = jax.ShapeDtypeStruct
+    outs = [S((256, DD), f32), S((256, DE), f32), S((4, DE + DD), f32)]
+    outs += [S((256, n), bf16) for _, n in ACTS] + [S((256, n), bf16) for n in GRADS]
+    V = pltpu.VMEM
+    scratch = [V((HE, 256, 256), f32), V((HD, 256, 256), f32), V((256, FFE), f32), V((256, FFD), f32),
+               V((256, 3 * DE), bf16), V((256, 3 * DD), bf16), V((256, DE), bf16), V((256, DD), bf16),
+               V((2, DE // 2, DE), bf16), V((2, DD // 2, DD), bf16),
+               V((256, DE), f32), V((256, DE), f32), V((256, DD), f32), V((256, DD), f32)] + [V((256, 1), f32)] * 4 + [
+               V((256, DE), f32), V((256, DD), f32), V((256, DE), f32), V((256, DD), f32)]
+    spec = pl.BlockSpec(memory_space=pltpu.VMEM)
+    args = (tokens, pos.T, tile[None, :], tile[:, None], gains, biases, cot, jnp.asarray(position_table()),
+            full.reshape(2, 16, full.shape[-2], 128))
+    return pl.pallas_call(
+        partial(chain_kernel, table), out_shape=outs, in_specs=[spec] * len(args), out_specs=[spec] * len(outs),
+        scratch_shapes=scratch, compiler_params=pltpu.CompilerParams(vmem_limit_bytes=62 << 20), name="chain",
+        cost_estimate=pl.CostEstimate(flops=11_000_000_000, bytes_accessed=40_000_000, transcendentals=5_000_000),
+    )(*args)
+
+
+def grad_panels(table, m, act, grad, turned, put):
+    mat = table[m]
+    rb, panels, padded = mat[0], mat[1], mat[5]
+    count = act.shape[1]
+
+    def turn(i, _):
+        turned[pl.ds(pl.multiple_of(i * 128, 128), 128), :] = act[:, lanes(i)].T
+        return 0
+
+    lax.fori_loop(0, count // 128, turn, 0)
+
+    def place(t, g, v):
+        if padded > rb:
+            v = v.reshape(16, rb, 128)
+            v = jnp.concatenate([v, jnp.zeros((16, padded - rb, 128), jnp.float32)], axis=1).astype(jnp.bfloat16)
         else:
-            m = m.reshape(16, rb, 2, panels, PANEL).transpose(2, 0, 3, 1, 4)
-        if padded > rb:
-            m = jnp.pad(m, ((0, 0), (0, 0), (0, 0), (0, padded - rb), (0, 0)))
-        out.append(m.reshape(2, 16, panels * padded, PANEL))
-    out = jnp.concatenate(out, axis=2)
-    return out.reshape(2, 4, 2, 2, out.shape[2], PANEL)
-
-
-def whole_attention(n1, w_qkv, heads, size, mask):
-    length = n1.shape[0]
-    proj = jnp.dot(n1, w_qkv, preferred_element_type=jnp.float32).astype(jnp.bfloat16)
-    proj = proj.reshape(length, 2, 3, heads // 2, size)
-    q, k, v = (proj[:, :, i].reshape(length, heads, size) for i in range(3))
-    z = jnp.einsum("qhd,khd->hqk", q, k, preferred_element_type=jnp.float32) * size ** (-0.5) + mask[None]
-    e = jnp.exp(z - jnp.max(z, axis=-1, keepdims=True))
-    p = e / jnp.sum(e, axis=-1, keepdims=True)
-    a = jnp.einsum("hqk,khd->qhd", p.astype(jnp.bfloat16), v, preferred_element_type=jnp.float32)
-    return a.astype(jnp.bfloat16).reshape(length, heads * size), (q, k, v, p)
-
-
-def whole_forward(x, mats, gains, biases, heads, size, mask):
-    w_qkv, w_out, w_in, w_down = mats
-    n1, s1 = norm_forward(x, gains[0], biases[0])
-    n1 = n1.astype(jnp.bfloat16)
-    a, att = whole_attention(n1, w_qkv, heads, size, mask)
-    x1 = x + jnp.dot(a, w_out, preferred_element_type=jnp.float32)
-    n2, s2 = norm_forward(x1, gains[1], biases[1])
-    n2 = n2.astype(jnp.bfloat16)
-    h = jnp.dot(n2, w_in, preferred_element_type=jnp.float32)
-    u = jax.nn.gelu(h, approximate=False).astype(jnp.bfloat16)
-    return x1 + jnp.dot(u, w_down, preferred_element_type=jnp.float32), (n1, s1, a, att, n2, s2, h, u)
-
-
-def whole_backward(dr, mats, gains, saved, heads, size):
-    w_qkv, w_out, w_in, w_down = mats
-    n1, s1, a, (q, k, v, p), n2, s2, h, u = saved
-    length = dr.shape[0]
-    r = dr.astype(jnp.bfloat16)
-    d_down = inner_rows(u, r)
-    du = times_transpose(r, w_down)
-    dh = jax.vjp(partial(jax.nn.gelu, approximate=False), h)[1](du)[0].astype(jnp.bfloat16)
-    d_in = inner_rows(n2, dh)
-    dn2 = times_transpose(dh, w_in)
-    dx1, dg2, db2 = norm_backward(dn2, s2, gains[1])
-    dx1 = dr + dx1
-    r1 = dx1.astype(jnp.bfloat16)
-    d_out = inner_rows(a, r1)
-    da = times_transpose(r1, w_out).astype(jnp.bfloat16).reshape(length, heads, size)
-    dp = jnp.einsum("qhd,khd->hqk", da, v, preferred_element_type=jnp.float32)
-    dv = jnp.einsum("hqk,qhd->khd", p.astype(jnp.bfloat16), da, preferred_element_type=jnp.float32)
-    dz = (p * (dp - jnp.sum(p * dp, axis=-1, keepdims=True))).astype(jnp.bfloat16)
-    dq = jnp.einsum("hqk,khd->qhd", dz, k, preferred_element_type=jnp.float32) * size ** (-0.5)
-    dk = jnp.einsum("hqk,qhd->khd", dz, q, preferred_element_type=jnp.float32) * size ** (-0.5)
-    half = heads // 2
-    dproj = jnp.stack([g.reshape(length, 2, half, size) for g in (dq, dk, dv)], axis=2)
-    dproj = dproj.astype(jnp.bfloat16).reshape(length, 3 * heads * size)
-    d_qkv = inner_rows(n1, dproj)
-    dn1 = times_transpose(dproj, w_qkv)
-    dx, dg1, db1 = norm_backward(dn1, s1, gains[0])
-    return dx1 + dx, [d_qkv, d_out, d_in, d_down], (dg1, dg2, db1, db2)
+            v = v.astype(jnp.bfloat16).reshape(16, rb, 128)
+        put(t, g, v)
+
+    if m in BY_ROWS:
+        half = count // 2
+
+        def body(i, _):
+            t, g = i // (panels // 2), i % (panels // 2)
+            v = dot(turned[pl.ds(pl.multiple_of(t * half, 128), half), :], grad[:, lanes(g, 256)])
+            place(t, 2 * g, v[:, :128])
+            place(t, 2 * g + 1, v[:, 128:])
+            return 0
+
+        lax.fori_loop(0, panels, body, 0)
+    else:
+        def body(g, _):
+            d = jnp.concatenate([grad[:, lanes(g)], grad[:, lanes(panels + g)]], axis=1)
+            v = dot(turned[:count, :], d)
+            place(0, g, v[:, :128])
+            place(1, g, v[:, 128:])
+            return 0
+
+        lax.fori_loop(0, panels, body, 0)
+
+
+def grads_kernel(table, *refs):
+    acts, grads, out, turned = refs[:9], refs[9:18], refs[18], refs[19]
+    for m in range(9):
+        at, padded = table[m][4], table[m][5]
+
+        def put(t, g, v):
+            out[t, :, pl.ds(pl.multiple_of(at + g * padded, 16), padded), :] = v
+
+        grad_panels(table, m, acts[m], grads[m], turned, put)
+
+
+def weight_grads(acts, grads, table, rows):
+    spec = pl.BlockSpec(memory_space=pltpu.VMEM)
+    return pl.pallas_call(
+        partial(grads_kernel, table), out_shape=jax.ShapeDtypeStruct((2, 16, rows, 128), jnp.bfloat16),
+        in_specs=[spec] * 18, out_specs=spec, scratch_shapes=[pltpu.VMEM((FFE, 256), jnp.bfloat16)],
+        compiler_params=pltpu.CompilerParams(vmem_limit_bytes=62 << 20), name="weight_grads",
+        cost_estimate=pl.CostEstimate(flops=5_500_000_000, bytes_accessed=32_000_000, transcendentals=0),
+    )(*acts, *grads)
 
 
 def swap(v):
@@ -831,25 +1151,12 @@
     parts = parts.at[jnp.where(used, place, 16 * SHARD_UNITS)].set(master.astype(jnp.bfloat16), mode="drop", unique_indices=True)
     shard = reduce_scatter(parts.reshape(4, 2, 2, SHARD_UNITS, 512), PLAN_DP, False, 1)
     full = gather(to_panels(shard, table), PLAN_ALL, True, 2)
-    mats = unpack(full, table)
-
-    mask = jnp.where(tile[:, None] == tile[None, :], 0.0, MASK_FILL).astype(jnp.float32)
-    x0 = tokens.astype(jnp.float32) + sincos_embed(pos, DE)
-    x2, enc = whole_forward(x0, mats[0:4], norm_gains[:, :DE], norm_biases[:, :DE], HE, HDE, mask)
-    e = x2.astype(jnp.bfloat16)
-    y0 = jnp.dot(e, mats[4], preferred_element_type=jnp.float32).astype(jnp.bfloat16).astype(jnp.float32) + sincos_embed(pos, DD)
-    decoded, dec = whole_forward(y0, mats[5:9], norm_gains[:, DE:], norm_biases[:, DE:], HD, HDD, mask)
-    dy0, dec_grads, dec_norm = whole_backward(cot, mats[5:9], norm_gains[:, DE:], dec, HD, HDD)
-    de = dy0.astype(jnp.bfloat16)
-    d_embed = inner_rows(e, de)
-    dx2 = times_transpose(de, mats[4])
-    dx0, enc_grads, enc_norm = whole_backward(dx2, mats[0:4], norm_gains[:, :DE], enc, HE, HDE)
-
-    grads = pack(enc_grads + [d_embed] + dec_grads, table)
-    summed = reduce_scatter(grads, PLAN_ALL, True, 3)
+    kept = chain(tokens, pos, tile, norm_gains, norm_biases, cot, full, table)
+    decoded, dx0, norms = kept[:3]
+    grads = weight_grads(kept[3:12], kept[12:21], table, full.shape[-2])
+    summed, norm_total = reduce_scatter(grads.reshape(full.shape), PLAN_ALL, True, 3, norms)
     spread_out = gather(from_panels(summed, table), PLAN_DP, False, 4).reshape(16 * SHARD_UNITS, 512)
     reduced = jnp.where(used[:, None], jnp.take(spread_out, jnp.clip(place, 0, 16 * SHARD_UNITS - 1), axis=0).astype(jnp.float32), 0.0)
-    norm_total = lax.psum(jnp.concatenate([jnp.stack(enc_norm), jnp.stack(dec_norm)], axis=1), ("dp", "tensor"))
     new_master, new_first, new_second = adamw(master, reduced, first_moment, second_moment, WEIGHT_DECAY, LEARN_RATE)
     norm_params = jnp.concatenate([norm_gains, norm_biases], axis=0)
     new_norms, norm_one_new, norm_two_new = adamw(norm_params, norm_total, norm_first, norm_second, 0.0, NORM_RATE)

time: 752 us -> 536 us (0.71)
  local copies, waits for them, and re-layouts: 221 us -> 32 us
  Pallas kernels: 348 us -> 462 us
  matrix products: 81.7 us -> 0.81 us
  blocking collectives: 38.7 us -> 0 us
  other arithmetic: 44.2 us -> 31.5 us
    pallas_call x2 -> x4, Pallas kernels: 161 us -> 271 us  [the longest x2 176 us: reduce_scatter(): pl.pallas_call(partial(reduce_kernel, plan, with_x, small is not None), o...]
    reshape x17 -> x0, local copies, waits for them, and re-layouts: 76.2 us -> none  [the longest x5 27.9 us: unpack(): m = m.transpose(1, 3, 0, 2, 4).reshape(16 * rb, 2 * panels * PANEL)]
    dot_general x37 -> x0, matrix products: 72.4 us -> none  [the longest x9 20.6 us: inner_rows(): lax.dot_general(left_side, right_side, (((0,), (0,)), ((), ())), preferre...]
    transpose x14 -> x0, local copies, waits for them, and re-layouts: 51.5 us -> none  [the longest x5 15.8 us: unpack(): m = m.transpose(0, 1, 3, 2, 4).reshape(2 * 16 * rb, panels * PANEL)]
    psum x1 -> x0, blocking collectives: 38.7 us -> none  [sequence_device(): lax.psum(jnp.concatenate([jnp.stack(enc_norm), jnp.stack(dec_norm)], axis...]
    unnamed x198 -> x40, local copies, waits for them, and re-layouts: 31.5 us -> 1.1 us
    slice x11 -> x0, local copies, waits for them, and re-layouts: 26.6 us -> none  [the longest x6 20.6 us: unpack(): full[:, :, at:at + panels * padded].reshape(2, 16, panels, padded, PANEL)]
    sub x2 -> x0, matrix products: 8.56 us -> none  [whole_attention(): e = jnp.exp(z - jnp.max(z, axis=-1, keepdims=True))]
  transfers between devices with their start and end apart: 5 -> 5, of which waited for: 0 -> 0; matrix products, arithmetic and copies ran while one was open for 45% -> 10% of each run, Pallas kernels for 47% -> 52%
where the time goes in v2:
time: 536 us; the launch traced here: 533 us
  Pallas kernels  462 us (86%)
  local copies, waits for them, and re-layouts  32 us (6%)
  other arithmetic  31.5 us (6%)
    pallas_call x2, Pallas kernels, gather(): pl.pallas_call(partial(gather_kernel, plan, with_x), out_shape=jax.ShapeD...  191 us
    pallas_call x2, Pallas kernels, reduce_scatter(): pl.pallas_call(partial(reduce_kernel, plan, with_x, small is not None), o...  176 us
    pallas_call x1, Pallas kernels, chain(): pl.pallas_call(partial(chain_kernel, table), out_shape=outs, in_specs=[sp...  62.5 us
    pallas_call x1, Pallas kernels, weight_grads(): pl.pallas_call(partial(grads_kernel, table), out_shape=jax.ShapeDtypeStru...  32.1 us
    scatter x1, other arithmetic, sequence_device(): parts.at[jnp.where(used, place, 16 * SHARD_UNITS)]  14.9 us
    gather x1, local copies, waits for them, and re-layouts, sequence_device(): jnp.take(spread_out, jnp.clip(place, 0, 16 * SHARD_UNITS - 1), axis=0)  11 us
  transfers between devices with their start and end apart: 5, of which 0 were waited for; matrix products, arithmetic and copies ran while one was open for 10% of the time, Pallas kernels for 52%

profile of v2, /device:TPU:1, one launch (start us, length us, event | category | flops | bytes accessed | tf_op | source)
XLA Modules:
  0.0 533.0 jit_solution(3783468464938008221)
XLA Ops:
  0.6 0.8 constant_dynamic-slice_fusion.4
  1.4 2.1 collective-permute-start.1
  3.5 0.9 dynamic-slice_bitcast_fusion.1
  4.4 0.1 collective-permute-start
  4.5 1.0 dynamic-slice_bitcast_fusion
  5.5 1.5 collective-permute-start.2
  7.0 0.9 compare_reduce_fusion
  7.9 0.1 fusion.7
  8.1 0.2 fusion.8
  8.2 0.1 select_reduce_fusion.1
  8.4 0.6 slice.64
  9.0 0.1 convert_reduce_fusion
  9.1 0.2 select_reduce_fusion
  9.3 0.7 fusion.5
  9.9 0.8 compare_and_fusion
  10.7 1.0 fusion.75
  11.7 14.9 %scatter_custom_fusion = bf16[10496,512]{1,0:T(8,128)(2,1)} fusion(s32[1296]{0:T(1024)S(1)} %get-tuple-element.55, bf16[]{:T(256)} %constant.217.clone.1, f32[1296,512]{1,0:T(8,128)} %param.17), kind=kCustom, calls=%fused_computation.2 | custom fusion | flops 663552 | bytes 13402114 | tf_op jit(solution)/shard_map/scatter | solution.py:1151
  26.7 83.6 %reduce_1.1 = bf16[656,512]{1,0:T(8,128)(2,1)} custom-call(bf16[4,2,2,656,512]{4,3,2,1,0:T(8,128)(2,1)} %bitcast.111), custom_call_target="tpu_custom_call" | custom-call | tf_op jit(solution)/shard_map/reduce_1/pallas_call | solution.py:698
  110.2 0.7 copy_bitcast_fusion.10
  111.0 0.7 slice.69
  111.7 0.8 slice.66
  112.5 0.8 slice.70
  113.3 0.9 slice.65
  114.2 0.9 slice_bitcast_fusion
  115.1 1.0 fusion.83
  116.3 0.1 reshape.861
  116.3 0.1 reshape.851
  116.5 0.1 reshape.857
  116.8 0.2 reshape.855
  117.2 0.6 fusion.76
  117.8 0.8 copy.112.tile_c
  118.6 95.6 %gather_2.1 = bf16[2,4,2,2,2640,128]{5,4,3,2,1,0:T(8,128)(2,1)} custom-call(bf16[2640,128]{1,0:T(8,128)(2,1)} %copy-done.1), custom_call_target="tpu_custom_call" | custom-call | tf_op jit(solution)/shard_map/gather_2/pallas_call | solution.py:541
  214.3 0.8 copy.102
  215.1 0.8 pad_maximum_fusion.3.tok
  216.0 0.8 pad_maximum_fusion.1.cot
  216.8 62.5 %chain.1 = (f32[256,512]{1,0:T(8,128)}, f32[256,768]{1,0:T(8,128)}, f32[4,1280]{1,0:T(4,128)}, bf16[256,768]{1,0:T(8,128)(2,1)}, bf16[256,768]{1,0:T(8,128)(2,1)...) custom-call(bf16[256,768]{1,0:T(8,128)(2,1)} %pad_maximum_fusion.3.t, ...), custom_call_target="tpu_custom_call" | custom-call | flops 11000000512 | bytes 40000000 | tf_op jit(solution)/shard_map/chain/pallas_call | solution.py:1054
  279.3 32.1 %weight_grads.1 = bf16[2,16,2640,128]{3,2,1,0:T(8,128)(2,1)} custom-call(bf16[256,768]{1,0:T(8,128)(2,1)} %get-tuple-element.33.refs_0_, bf16[256,768]{1,0:T(8,128)(2,1)} %get-tuple-element.34.refs_1_, bf16[256,768]{1,0:T(8,128)(2,1)} %get-tuple-element.35.refs_2_, bf16[256,3072]{1,0:T(8,128)(2,1)} %get-tuple-element.36.refs_3_, ...), custom_call_target="tpu_custom_call" | custom-call | flops 5500000256 | bytes 32000000 | tf_op jit(solution)/shard_map/weight_grads/pallas_call | solution.py:1115
  311.4 92.8 %reduce_3.1 = (bf16[2640,128]{1,0:T(8,128)(2,1)}, f32[4,1280]{1,0:T(4,128)}) custom-call(bf16[2,4,2,2,2640,128]{5,4,3,2,1,0:T(8,128)(2,1)} %bitcast.110, f32[4,1280]{1,0:T(4,128)} %get-tuple-element.51.rest_0_), custom_call_target="tpu_custom_call" | custom-call | tf_op jit(solution)/shard_map/reduce_3/pallas_call | solution.py:698
  404.2 0.7 slice.81
  404.9 0.7 slice.79
  405.6 0.8 fusion.81
  406.5 0.9 slice.74
  407.4 0.9 fusion.80
  408.3 1.0 fusion.82
  409.3 0.7 constant_dynamic-slice_fusion.1
  410.0 0.5 collective-permute-start.3
  410.5 0.8 constant_dynamic-slice_fusion
  411.3 1.0 collective-permute-start.4
  412.4 0.1 reshape.882
  412.6 0.1 reshape.872
  412.7 0.1 copy.121
  412.9 0.2 reshape.876
  413.1 0.1 copy.144
  413.1 0.1 reshape.878
  413.3 0.3 concatenate.22
  413.6 0.9 pad.9.mine
  414.5 95.3 %gather_4.1 = bf16[4,2,2,656,512]{4,3,2,1,0:T(8,128)(2,1)} custom-call(bf16[656,512]{1,0:T(8,128)(2,1)} %pad.9.mine), custom_call_target="tpu_custom_call" | custom-call | tf_op jit(solution)/shard_map/gather_4/pallas_call | solution.py:541
  509.9 11.0 %gather_fusion = bf16[1296,512]{1,0:T(8,128)(2,1)} fusion(bf16[10496,512]{1,0:T(8,128)(2,1)} %bitcast.112, s32[2048]{0:T(1024)S(1)} %pad_clamp_fusion), kind=kCustom, calls=%fused_computation | custom fusion | bytes 2659392 | tf_op jit(solution)/shard_map/jit(_take)/gather | solution.py:1159
  520.9 7.2 %multiply_subtract_fusion = (f32[1296,512]{1,0:T(8,128)}, f32[1296,512]{1,0:T(8,128)}, f32[1296,512]{1,0:T(8,128)}) fusion(f32[1296,512]{1,0:T(8,128)S(1)} %copy-done, bf16[1296,512]{1,0:T(8,128)(2,1)} %gather_fusion, pred[1296]{0:T(1024)(128)(4,1)S(1)} %get-tuple-element.62, pred[1296]{0:T(1024)(128)(4,1)S(1)} %get-tuple-element.115, f32[1296,512]{1,0:T(8,128)} %param.18, ...), kind=kLoop, calls=%fused_computation.7 | loop fusion | flops 11280384 | bytes 17254944 | tf_op jit(solution)/shard_map/sub | solution.py:92
  528.1 0.7 multiply_subtract_fusion.1
  528.8 1.0 select_bitcast_fusion.3
  529.8 0.8 pad_maximum_fusion.2
  530.6 1.1 select_bitcast_fusion.1
  531.7 0.9 pad_maximum_fusion
  (74 shorter events, 0.9 us)
Async XLA Ops:
  1.4 212.8 %collective-permute-start.1 = (s32[3,128]{1,0:T(4,128)S(1)}, s32[3,128]{1,0:T(4,128)S(1)}, u32[]{:S(2)}, u32[]{:S(2)}) collective-permute-start(s32[3,128]{1,0:T(4,128)S(1)} %bitcast.149), channel_id=1, source_target_pairs={{0,1},{1,0},{2,3},{3,2},{4,5},{5,4},{6,7},{7,6},{8,9},{9,8},{10,11... | collective-permute-start | bytes 4616 | tf_op jit(solution)/shard_map/ppermute | solution.py:1124
  4.4 210.6 %collective-permute-start = (bf16[128,768]{1,0:T(8,128)(2,1)S(1)}, bf16[128,768]{1,0:T(8,128)(2,1)S(1)}, u32[]{:S(2)}, u32[]{:S(2)}) collective-permute-start(bf16[128,768]{1,0:T(8,128)(2,1)S(1)} %dynamic-slice_bitcast_fusion.1), channel_id=1, source_target_pairs={{0,1},{1,0},{2,3},{3,2},{4,5},{5,4},{6,7},{7,6},{8,9},{9,8},{10,11... | collective-permute-start | bytes 589832 | tf_op jit(solution)/shard_map/ppermute | solution.py:1124
  5.5 210.4 %collective-permute-start.2 = (f32[128,512]{1,0:T(8,128)S(1)}, f32[128,512]{1,0:T(8,128)S(1)}, u32[]{:S(2)}, u32[]{:S(2)}) collective-permute-start(f32[128,512]{1,0:T(8,128)S(1)} %dynamic-slice_bitcast_fusion), channel_id=1, source_target_pairs={{0,1},{1,0},{2,3},{3,2},{4,5},{5,4},{6,7},{7,6},{8,9},{9,8},{10,11... | collective-permute-start | bytes 786440 | tf_op jit(solution)/shard_map/ppermute | solution.py:1124
  114.2 2.9 copy-start.12
  117.2 1.4 copy-start.1
  118.6 96.5 %copy-start.6 = (bf16[2,128,768]{2,1,0:T(8,128)(2,1)S(1)}, bf16[2,128,768]{2,1,0:T(8,128)(2,1)}, u32[]{:S(2)}) copy-start(bf16[2,128,768]{2,1,0:T(8,128)(2,1)} %param.13) | copy-start | bytes 1179652
  118.6 97.3 %copy-start.3 = (f32[2,128,512]{2,1,0:T(8,128)S(1)}, f32[2,128,512]{2,1,0:T(8,128)}, u32[]{:S(2)}) copy-start(f32[2,128,512]{2,1,0:T(8,128)} %param.24) | copy-start | bytes 1572868
  311.4 97.9 %copy-start.4 = (f32[256,512]{1,0:T(8,128)S(1)}, f32[256,512]{1,0:T(8,128)}, u32[]{:S(2)}) copy-start(f32[256,512]{1,0:T(8,128)} %get-tuple-element.31) | copy-start | bytes 1572868
  311.4 99.1 %copy-start.2 = (f32[256,768]{1,0:T(8,128)S(1)}, f32[256,768]{1,0:T(8,128)}, u32[]{:S(2)}) copy-start(f32[256,768]{1,0:T(8,128)} %get-tuple-element.32) | copy-start | bytes 2359300
  410.0 118.8 %collective-permute-start.3 = (f32[128,512]{1,0:T(8,128)}, f32[128,512]{1,0:T(8,128)}, u32[]{:S(2)}, u32[]{:S(2)}) collective-permute-start(f32[128,512]{1,0:T(8,128)} %constant_dynamic-slice_fusion.1), channel_id=1, source_target_pairs={{0,1},{1,0},{2,3},{3,2},{4,5},{5,4},{6,7},{7,6},{8,9},{9,8},{10,11... | collective-permute-start | bytes 786440 | tf_op jit(solution)/shard_map/ppermute | solution.py:1124
  411.3 119.3 %collective-permute-start.4 = (f32[128,768]{1,0:T(8,128)}, f32[128,768]{1,0:T(8,128)}, u32[]{:S(2)}, u32[]{:S(2)}) collective-permute-start(f32[128,768]{1,0:T(8,128)} %constant_dynamic-slice_fusion), channel_id=1, source_target_pairs={{0,1},{1,0},{2,3},{3,2},{4,5},{5,4},{6,7},{7,6},{8,9},{9,8},{10,11... | collective-permute-start | bytes 1179656 | tf_op jit(solution)/shard_map/ppermute | solution.py:1124
  509.9 11.0 %copy-start = (f32[1296,512]{1,0:T(8,128)S(1)}, f32[1296,512]{1,0:T(8,128)}, u32[]{:S(2)}) copy-start(f32[1296,512]{1,0:T(8,128)} %param.17) | copy-start | bytes 7962628
  520.9 7.2 %copy-start.7 = (f32[4,1280]{1,0:T(4,128)S(1)}, f32[4,1280]{1,0:T(4,128)}, u32[]{:S(2)}) copy-start(f32[4,1280]{1,0:T(4,128)} %param.22) | copy-start | bytes 61444
  520.9 7.2 %copy-start.8 = (f32[4,1280]{1,0:T(4,128)S(1)}, f32[4,1280]{1,0:T(4,128)}, u32[]{:S(2)}) copy-start(f32[4,1280]{1,0:T(4,128)} %param.23) | copy-start | bytes 61444
  520.9 7.2 %copy-start.9 = (f32[4,1280]{1,0:T(4,128)S(1)}, f32[4,1280]{1,0:T(4,128)}, u32[]{:S(2)}) copy-start(f32[4,1280]{1,0:T(4,128)} %get-tuple-element.53) | copy-start | bytes 61444
  520.9 7.2 %copy-start.10 = (f32[2,1280]{1,0:T(2,128)S(1)}, f32[2,1280]{1,0:T(2,128)}, u32[]{:S(2)}) copy-start(f32[2,1280]{1,0:T(2,128)} %gains.1) | copy-start | bytes 30724
  520.9 7.2 %copy-start.11 = (f32[2,1280]{1,0:T(2,128)S(1)}, f32[2,1280]{1,0:T(2,128)}, u32[]{:S(2)}) copy-start(f32[2,1280]{1,0:T(2,128)} %biases.1) | copy-start | bytes 30724
  520.9 7.9 %copy-start.5 = (f32[256,512]{1,0:T(8,128)S(1)}, f32[256,512]{1,0:T(8,128)}, u32[]{:S(2)}) copy-start(f32[256,512]{1,0:T(8,128)} %get-tuple-element.31) | copy-start | bytes 1572868

commit v3 on v2

--- a/solution.py
+++ b/solution.py
@@ -473,82 +473,6 @@
 BACK = {"z+": "z-", "z-": "z+", "x": "x", "y": "y"}
 
 
-def gather_kernel(plan, with_x, mine, out, send, recv, sib_send, sib_recv, own_sem):
-    p = Place()
-    p.greet(["c", "y", "x"] if with_x else ["c", "y"])
-    trees = [spread(o) for o, _, _ in plan]
-    ids = [{d: i + 32 * g for i, d in enumerate(sorted(t))} for g, t in enumerate(trees)]
-    waits = []
-
-    def at(disp, core, g):
-        t, z, y = p.at(disp)
-        return out.at[((t,) if with_x else ()) + (z, y, core, pl.ds(plan[g][1], plan[g][2]))]
-
-    def push(src, g, nd, way, cond):
-        k = ids[g][nd]
-        od = None
-        cp = pltpu.make_async_remote_copy(src_ref=src[0], dst_ref=src[1], send_sem=send.at[k], recv_sem=recv.at[k],
-                                          device_id=p.ids[way], device_id_type=MESH)
-        c2 = cond
-        if way == "z+":
-            c2 = both(cond, p.z < 3)
-        elif way == "z-":
-            c2 = both(cond, p.z > 0)
-        when(c2, cp.start)
-        waits.append((c2, cp))
-
-    def share(src, g, disp, cond):
-        k = ids[g][disp]
-        cp = pltpu.make_async_remote_copy(src_ref=src, dst_ref=at(disp, p.c, g), send_sem=sib_send.at[k], recv_sem=sib_recv.at[k],
-                                          device_id=p.ids["c"], device_id_type=MESH)
-        when(cond, cp.start)
-        waits.append((cond, cp))
-
-    zero = (0, 0, 0)
-    for g, tree in enumerate(trees):
-        src = mine.at[pl.ds(plan[g][1], plan[g][2])]
-        for nd, way in tree[zero]:
-            push((src, at(zero, p.c, g)), g, nd, way, None)
-    own = pltpu.make_async_copy(mine, out.at[((p.x,) if with_x else ()) + (p.z, p.y, p.c)], own_sem)
-    own.start()
-    for g in range(len(plan)):
-        share(mine.at[pl.ds(plan[g][1], plan[g][2])], g, zero, None)
-    events = sorted((hops(d), g, d) for g, t in enumerate(trees) for d in t if d != zero)
-    for _, g, d in events:
-        cond = p.there(d)
-        blk = at(d, p.c, g)
-        got = pltpu.make_async_remote_copy(src_ref=blk, dst_ref=blk, send_sem=send.at[ids[g][d]], recv_sem=recv.at[ids[g][d]],
-                                           device_id=p.ids["c"], device_id_type=MESH)
-        when(cond, got.wait_recv)
-        for nd, way in trees[g][d]:
-            push((blk, blk), g, nd, way, cond)
-        share(blk, g, d, cond)
-    for g, t in enumerate(trees):
-        for d in t:
-            blk = at(d, 1 - p.c, g)
-            got = pltpu.make_async_remote_copy(src_ref=blk, dst_ref=blk, send_sem=sib_send.at[ids[g][d]], recv_sem=sib_recv.at[ids[g][d]],
-                                               device_id=p.ids["c"], device_id_type=MESH)
-            when(p.there(d), got.wait_recv)
-    own.wait()
-    for c, cp in waits:
-        when(c, cp.wait_send)
-
-
-def gather(shard, plan, with_x, ident, space=pl.ANY):
-    rows, width = shard.shape
-    lead = (2, 4, 2, 2) if with_x else (4, 2, 2)
-    sems = pltpu.SemaphoreType.DMA((32 * len(plan),))
-    return pl.pallas_call(
-        partial(gather_kernel, plan, with_x),
-        out_shape=jax.ShapeDtypeStruct(lead + (rows, width), shard.dtype),
-        in_specs=[pl.BlockSpec(memory_space=space)],
-        out_specs=pl.BlockSpec(memory_space=space),
-        scratch_shapes=[sems, sems, sems, sems, pltpu.SemaphoreType.DMA],
-        compiler_params=pltpu.CompilerParams(collective_id=ident, has_side_effects=True, vmem_limit_bytes=60 << 20),
-        name=f"gather_{ident}",
-    )(shard)
-
-
 def add_rows(acc, got, step=80):
     n = acc.shape[0]
     while n % step:
@@ -562,173 +486,31 @@
     lax.fori_loop(0, n // step, body, 0)
 
 
-def total_steps(p, src, out, mid, line, send, recv):
-    waits = []
-
-    def move(k, a, b, way, cond=None):
-        cp = pltpu.make_async_remote_copy(src_ref=a, dst_ref=b, send_sem=send.at[k], recv_sem=recv.at[k],
-                                          device_id=p.ids[way], device_id_type=MESH)
-        when(cond, cp.start)
-        waits.append((cond, cp))
-
-    def land(k, b, cond=None):
-        when(cond, pltpu.make_async_remote_copy(src_ref=b, dst_ref=b, send_sem=send.at[k], recv_sem=recv.at[k],
-                                                device_id=p.ids["c"], device_id_type=MESH).wait_recv)
-
-    now = src
-    for k, way in enumerate(("c", "x", "y")):
-        move(k, now, mid.at[k], way)
-        yield
-        land(k, mid.at[k])
-        nxt = mid.at[3 + k] if k < 2 else line.at[p.z]
-        nxt[...] = now[...] + mid[k]
-        now = nxt
-    for k in range(3):
-        lo, hi = jnp.maximum(p.z - k, 0), jnp.minimum(p.z + k, 3)
-        if k > 0:
-            land(2 + k, line.at[lo], p.z >= k)
-            land(5 + k, line.at[hi], p.z + k <= 3)
-        move(3 + k, line.at[lo], line.at[lo], "z+", jnp.logical_and(p.z >= k, p.z < 3))
-        move(6 + k, line.at[hi], line.at[hi], "z-", jnp.logical_and(p.z + k <= 3, p.z > 0))
-        yield
-    land(5, line.at[jnp.maximum(p.z - 3, 0)], p.z >= 3)
-    land(8, line.at[jnp.minimum(p.z + 3, 3)], p.z <= 0)
-    out[...] = (line[0] + line[1]) + (line[2] + line[3])
-    for c, cp in waits:
-        when(c, cp.wait_send)
-
-
-def reduce_kernel(plan, with_x, small, src, *rest):
-    n = len(plan)
-    steps = iter(())
-    if small:
-        small_src, out, small_out = rest[:3]
-        mid, line, small_send, small_recv = rest[-4:]
-        rest = rest[3:-4]
-    else:
-        out, rest = rest[0], rest[1:]
-    accs, halves, bufs = rest[:n], rest[n:2 * n], rest[2 * n:3 * n]
-    send, recv, sib_send, sib_recv, loads = rest[3 * n:]
-    p = Place()
-    p.greet(["c", "y", "x"] if with_x else ["c", "y"])
-    if small:
-        steps = total_steps(p, small_src, small_out, mid, line, small_send, small_recv)
-    trees = [spread(o) for o, _, _ in plan]
-    ids = [{d: i + 32 * g for i, d in enumerate(sorted(t))} for g, t in enumerate(trees)]
-    waits = []
-    zero = (0, 0, 0)
-
-    def ix(disp):
-        t, z, y = p.at(disp)
-        return ((t,) if with_x else ()) + (z, y)
-
-    events = sorted((-hops(d), g, d) for g, t in enumerate(trees) for d in t)
-    for _, g, d in events:
-        cond = p.there(d)
-        k = ids[g][d]
-        rows = pl.ds(plan[g][1], plan[g][2])
-        cp = pltpu.make_async_remote_copy(
-            src_ref=src.at[ix(d) + (1 - p.c, rows)], dst_ref=halves[g].at[ix(d)], send_sem=sib_send.at[k],
-            recv_sem=sib_recv.at[k], device_id=p.ids["c"], device_id_type=MESH)
-        ld = pltpu.make_async_copy(src.at[ix(d) + (p.c, rows)], accs[g].at[ix(d)], loads.at[k])
-
-        def go(cp=cp, ld=ld):
-            cp.start()
-            ld.start()
-        when(cond, go)
-        waits.append((cond, cp))
-    for number, (_, g, d) in enumerate(events):
-        k = ids[g][d]
-        rows = pl.ds(plan[g][1], plan[g][2])
-        if number % 8 == 0:
-            next(steps, None)
-
-        def step(g=g, d=d, k=k, rows=rows):
-            acc = accs[g].at[ix(d)]
-            pltpu.make_async_copy(src.at[ix(d) + (p.c, rows)], acc, loads.at[k]).wait()
-            half = halves[g].at[ix(d)]
-            pltpu.make_async_remote_copy(src_ref=half, dst_ref=half, send_sem=sib_send.at[k], recv_sem=sib_recv.at[k],
-                                         device_id=p.ids["c"], device_id_type=MESH).wait_recv()
-            add_rows(acc, half)
-            for nd, way in trees[g][d]:
-                kk = ids[g][nd]
-                buf = bufs[g].at[kk - 32 * g]
-
-                def take(acc=acc, buf=buf, kk=kk):
-                    pltpu.make_async_remote_copy(src_ref=buf, dst_ref=buf, send_sem=send.at[kk], recv_sem=recv.at[kk],
-                                                 device_id=p.ids["c"], device_id_type=MESH).wait_recv()
-                    add_rows(acc, buf)
-                if way == "z+":
-                    when(p.z < 3, take)
-                elif way == "z-":
-                    when(p.z > 0, take)
-                else:
-                    take()
-        cond = p.there(d)
-        when(cond, step)
-        if d != zero:
-            way = [w for t in trees[g].values() for nd, w in t if nd == d][0]
-            acc = accs[g].at[ix(d)]
-            cp = pltpu.make_async_remote_copy(src_ref=acc, dst_ref=bufs[g].at[k - 32 * g], send_sem=send.at[k], recv_sem=recv.at[k],
-                                              device_id=p.ids[BACK[way]], device_id_type=MESH)
-            when(cond, cp.start)
-            waits.append((cond, cp))
-        else:
-            out[rows, :] = accs[g][ix(d)]
-    for _ in steps:
-        pass
-    for c, cp in waits:
-        when(c, cp.wait_send)
-
-
-def reduce_scatter(whole, plan, with_x, ident, small=None):
-    rows, width = whole.shape[-2:]
-    dt = whole.dtype
-    lead = (2, 4, 2) if with_x else (4, 2)
-    blocks = [pltpu.VMEM(lead + (num, width), dt) for _, _, num in plan]
-    bufs = [pltpu.VMEM((len(spread(o)), num, width), dt) for o, _, num in plan]
-    sems = pltpu.SemaphoreType.DMA((32 * len(plan),))
-    vmem = pl.BlockSpec(memory_space=pltpu.VMEM)
-    out = jax.ShapeDtypeStruct((rows, width), dt)
-    scratch = blocks + blocks + bufs + [sems] * 5
-    if small is not None:
-        out = (out, jax.ShapeDtypeStruct(small.shape, small.dtype))
-        scratch += [pltpu.VMEM((5,) + small.shape, small.dtype), pltpu.VMEM((4,) + small.shape, small.dtype)]
-        scratch += [pltpu.SemaphoreType.DMA((9,))] * 2
-    return pl.pallas_call(
-        partial(reduce_kernel, plan, with_x, small is not None),
-        out_shape=out,
-        in_specs=[pl.BlockSpec(memory_space=pl.ANY)] + ([] if small is None else [vmem]),
-        out_specs=vmem if small is None else (vmem, vmem),
-        scratch_shapes=scratch,
-        compiler_params=pltpu.CompilerParams(collective_id=ident, has_side_effects=True, vmem_limit_bytes=62 << 20),
-        name=f"reduce_{ident}",
-    )(*((whole,) if small is None else (whole, small)))
-
-
-PLAN_ALL = [("zxy", 0, 640), ("zyx", 640, 640), ("xzy", 1280, 640), ("yzx", 1920, 720)]
-PLAN_DP = [("zy", 0, 656)]
 SHARD_UNITS = 656
 PANEL = 128
+GROUPS = ((0, 1), (2,), (3,), (4, 5, 6), (7, 8))
 
 
 def layout(shapes, shards):
     table = []
-    unit_at, row_at = 0, 0
-    for rows, cols in shapes:
+    unit_at, row_at, flat_at = 0, 0, 0
+    starts = [g[0] for g in GROUPS]
+    for i, (rows, cols) in enumerate(shapes):
+        if i in starts:
+            unit_at = -(-unit_at // 16) * 16
         rb, panels = rows // shards, cols // PANEL
         units = rb * cols // 512
         padded = -(-rb // 16) * 16
-        table.append((rb, panels, units, unit_at, row_at, padded))
+        table.append((rb, panels, units, unit_at, row_at, padded, flat_at))
         unit_at += units
         row_at += padded * panels
+        flat_at += units * shards
     return table, unit_at, row_at
 
 
 def unit_places(units, table, shards):
     place = jnp.zeros_like(units)
-    for rb, panels, n, first, _, _ in table:
-        lo = first * shards
+    for _, _, n, first, _, _, lo in table:
         v = units - lo
         here = (v // n) * SHARD_UNITS + first + v % n
         place = jnp.where(v >= 0, here, place)
@@ -751,25 +533,6 @@
     rank = (slot - before).astype(jnp.float32)
     at = jnp.sum((row <= rank[:, None]).astype(jnp.int32), axis=1)
     return block * 128 + at, slot < upto[count - 1]
-
-
-def to_panels(shard, table):
-    out = []
-    for rb, panels, n, first, _, padded in table:
-        m = shard[first:first + n].reshape(rb, panels, PANEL).transpose(1, 0, 2)
-        if padded > rb:
-            m = jnp.pad(m, ((0, 0), (0, padded - rb), (0, 0)))
-        out.append(m.reshape(panels * padded, PANEL))
-    return jnp.concatenate(out, axis=0)
-
-
-def from_panels(rows, table):
-    out = []
-    for rb, panels, n, first, at, padded in table:
-        m = rows[at:at + panels * padded].reshape(panels, padded, PANEL)[:, :rb]
-        out.append(m.transpose(1, 0, 2).reshape(n, 512))
-    out = jnp.concatenate(out, axis=0)
-    return jnp.pad(out, ((0, SHARD_UNITS - out.shape[0]), (0, 0)))
 
 
 BY_ROWS = (1, 3, 6, 8)
@@ -835,7 +598,7 @@
 
 
 def panel(w, t, mat, g, lo=0, num=16):
-    rb, _, _, _, at, padded = mat
+    rb, _, _, _, at, padded, _ = mat
     rows = pl.ds(pl.multiple_of(at + g * padded, 16), padded)
     v = w[t, lo:lo + num, rows, :] if isinstance(lo, int) else w[t, pl.ds(lo, num), rows, :]
     if padded > rb:
@@ -1099,25 +862,335 @@
         lax.fori_loop(0, panels, body, 0)
 
 
-def grads_kernel(table, *refs):
-    acts, grads, out, turned = refs[:9], refs[9:18], refs[18], refs[19]
-    for m in range(9):
-        at, padded = table[m][4], table[m][5]
-
-        def put(t, g, v):
-            out[t, :, pl.ds(pl.multiple_of(at + g * padded, 16), padded), :] = v
-
-        grad_panels(table, m, acts[m], grads[m], turned, put)
-
-
-def weight_grads(acts, grads, table, rows):
-    spec = pl.BlockSpec(memory_space=pltpu.VMEM)
+class Wires:
+    def __init__(self, place, sem):
+        self.place, self.sem, self.used, self.waits = place, sem, 0, []
+
+    def new(self, n=1):
+        self.used += n
+        assert self.used <= self.sem.shape[0], self.used
+        return self.used - n
+
+    def copy(self, k, src, dst, way):
+        return pltpu.make_async_remote_copy(src_ref=src, dst_ref=dst, send_sem=self.sem.at[k], recv_sem=self.sem.at[k + 1],
+                                            device_id=self.place.ids[way], device_id_type=MESH)
+
+    def send(self, k, src, dst, way, cond=None):
+        cp = self.copy(k, src, dst, way)
+        when(cond, cp.start)
+        self.waits.append((cond, cp))
+
+    def land(self, k, dst, cond=None):
+        when(cond, self.copy(k, dst, dst, "c").wait_recv)
+
+    def drain(self):
+        for cond, cp in self.waits:
+            when(cond, cp.wait_send)
+
+
+def edge_slot(p, parent, way):
+    dz, fy, _ = parent
+    if way == "z+":
+        return -dz
+    if way == "z-":
+        return 3 + dz
+    return 6 + p.z + dz if way == "y" else 10 + 4 * fy + p.z + dz
+
+
+def edge_slots(order):
+    return 18 if "x" in order else 10
+
+
+def beyond(p, way):
+    return p.z < 3 if way == "z+" else p.z > 0 if way == "z-" else None
+
+
+def reduce_events(p, w, order, own, half, bufs, done):
+    tree = spread(order)
+    top = max(hops(d) for d in tree)
+    with_x = "x" in order
+    pair = {d: w.new(2) for d in tree}
+    wire = {d: w.new(2) for d in tree}
+    parent = {nd: (d, way) for d, t in tree.items() for nd, way in t}
+    events = []
+    for d in sorted(tree, key=lambda d: (-hops(d), d)):
+        def act(d=d):
+            cond = p.there(d)
+
+            def step():
+                acc = own(d)
+                w.land(pair[d], half(d))
+                add_rows(acc, half(d))
+                for nd, way in tree[d]:
+                    buf = bufs.at[edge_slot(p, d, way)]
+
+                    def take(buf=buf, nd=nd):
+                        w.land(wire[nd], buf)
+                        add_rows(acc, buf)
+                    when(beyond(p, way), take)
+            when(cond, step)
+            if hops(d) == 0:
+                done()
+            else:
+                up, way = parent[d]
+                w.send(wire[d], own(d), bufs.at[edge_slot(p, up, way) if way[0] == "z" else edge_slot(p, d, way) if way == "y" else edge_slot(p, (d[0], d[1], 0), way)],
+                       BACK[way], cond)
+        events.append((top - hops(d), act))
+
+    def share(give):
+        for d in sorted(tree, key=lambda d: (-hops(d), d)):
+            w.send(pair[d], give(d), half(d), "c", p.there(d))
+
+    return events, share, top
+
+
+def gather_events(p, w, order, first, at):
+    tree = spread(order)
+    pair = {d: w.new(2) for d in tree}
+    wire = {d: w.new(2) for d in tree}
+    events = []
+    for d in sorted(tree, key=lambda d: (hops(d), d)):
+        def act(d=d):
+            cond = p.there(d)
+            blk = at(d, p.c)
+            if hops(d):
+                w.land(wire[d], blk, cond)
+                src = blk
+            else:
+                src = first
+            for nd, way in tree[d]:
+                w.send(wire[nd], src, blk, way, both(cond, beyond(p, way)))
+            w.send(pair[d], src, blk, "c", cond)
+        events.append((hops(d), act))
+
+    def finish():
+        for d in tree:
+            w.land(pair[d], at(d, 1 - p.c), p.there(d))
+
+    return events, finish
+
+
+def run_events(lists, stride, extra=iter(()), every=8):
+    todo = sorted(((level + stride * g, g, i), act) for g, evs in enumerate(lists) for i, (level, act) in enumerate(evs))
+    for n, (_, act) in enumerate(todo):
+        if n % every == 0:
+            next(extra, None)
+        act()
+    for _ in extra:
+        pass
+
+
+def group_span(table, mats):
+    first, last = table[mats[0]], table[mats[-1]]
+    units = last[3] + last[2] - first[3]
+    return first[3], -(-units // 16) * 16, first[4], last[4] + last[1] * last[5] - first[4]
+
+
+def units_to_panels(table, mats, units, flat, put):
+    base, count = table[mats[0]][3], units.shape[0]
+    for k in range(4):
+        flat[pl.ds(k, count, stride=4), :] = units[:, 128 * k:128 * (k + 1)].astype(jnp.float32)
+    for m in mats:
+        rb, panels, n, first, _, padded, _ = table[m]
+        for g in range(panels):
+            v = flat[pl.ds(4 * (first - base) + g, rb, stride=panels), :]
+            if padded > rb:
+                v = jnp.concatenate([v, jnp.zeros((padded - rb, 128), jnp.float32)], axis=0)
+            put(m, g, v.astype(jnp.bfloat16))
+
+
+def panels_to_units(table, mats, take, flat, units):
+    base, count = table[mats[0]][3], units.shape[0]
+    used = 0
+    for m in mats:
+        rb, panels, n, first, _, padded, _ = table[m]
+        for g in range(panels):
+            flat[pl.ds(4 * (first - base) + g, rb, stride=panels), :] = take(m, g)[:rb]
+        used = 4 * (first - base + n)
+    if used < 4 * count:
+        flat[used:4 * count, :] = jnp.zeros((4 * count - used, 128), jnp.float32)
+    for k in range(4):
+        units[:, 128 * k:128 * (k + 1)] = flat[pl.ds(k, count, stride=4), :].astype(jnp.bfloat16)
+
+
+def weights_kernel(table, groups, stride, parts, out, *rest):
+    n = len(groups)
+    accs, halves, bufs, shards = (rest[i * n:(i + 1) * n] for i in range(4))
+    flat, sem = rest[4 * n:]
+    p = Place()
+    p.greet(["c", "y", "x"])
+    w = Wires(p, sem)
+    lists, finishes = [], []
+    for g, mats in enumerate(groups):
+        u0, un, r0, rn = group_span(table, mats)
+        acc, half, buf, shard = accs[g], halves[g], bufs[g], shards[g]
+        load = w.new()
+        own_sem = w.new()
+
+        def start(u0=u0, un=un, acc=acc, load=load):
+            pltpu.make_async_copy(parts.at[:, :, p.c, pl.ds(u0, un)], acc, sem.at[load]).start()
+
+        def own(d, acc=acc):
+            return acc.at[p.at(d)[1:]]
+
+        def other(d, half=half):
+            return half.at[p.at(d)[1:]]
+
+        def done(g=g, mats=mats, acc=acc, shard=shard, r0=r0, rn=rn, own_sem=own_sem):
+            def put(m, i, v):
+                lo = table[m][4] - r0 + i * table[m][5]
+                shard[lo:lo + table[m][5], :] = v
+            units_to_panels(table, mats, acc.at[p.z, p.y], flat, put)
+            pltpu.make_async_copy(shard, out.at[p.x, p.z, p.y, p.c, pl.ds(r0, rn)], sem.at[own_sem]).start()
+
+        ev, share, top = reduce_events(p, w, "zy", own, other, buf, done)
+
+        def begin(start=start, share=share, u0=u0, un=un, acc=acc, load=load):
+            start()
+            share(lambda d: parts.at[p.at(d)[1:] + (1 - p.c, pl.ds(u0, un))])
+
+        def loaded(u0=u0, un=un, acc=acc, load=load):
+            pltpu.make_async_copy(parts.at[:, :, p.c, pl.ds(u0, un)], acc, sem.at[load]).wait()
+
+        def at(d, core, r0=r0, rn=rn):
+            t, z, y = p.at(d)
+            return out.at[t, z, y, core, pl.ds(r0, rn)]
+
+        ag, finish = gather_events(p, w, "zyx", shard, at)
+        evs = [(-1, begin), (-0.5, loaded)] + ev + [(top + 1 + lv, a) for lv, a in ag]
+        lists.append(evs)
+
+        def end(finish=finish, shard=shard, r0=r0, rn=rn, own_sem=own_sem):
+            finish()
+            pltpu.make_async_copy(shard, out.at[p.x, p.z, p.y, p.c, pl.ds(r0, rn)], sem.at[own_sem]).wait()
+
+        finishes.append(end)
+    run_events(lists, stride)
+    for f in finishes:
+        f()
+    w.drain()
+
+
+def spread_weights(parts, table, rows, groups, stride, ident):
+    spans = [group_span(table, m) for m in groups]
+    bf16 = jnp.bfloat16
+    scratch = [pltpu.VMEM((4, 2, s[1], 512), bf16) for s in spans] * 2
+    scratch += [pltpu.VMEM((edge_slots("zy"), s[1], 512), bf16) for s in spans]
+    scratch += [pltpu.VMEM((s[3], 128), bf16) for s in spans]
+    scratch += [pltpu.VMEM((4 * max(s[1] for s in spans), 128), jnp.float32), pltpu.SemaphoreType.DMA((len(groups) * (2 + 4 * 14 + 4 * 28),))]
     return pl.pallas_call(
-        partial(grads_kernel, table), out_shape=jax.ShapeDtypeStruct((2, 16, rows, 128), jnp.bfloat16),
-        in_specs=[spec] * 18, out_specs=spec, scratch_shapes=[pltpu.VMEM((FFE, 256), jnp.bfloat16)],
-        compiler_params=pltpu.CompilerParams(vmem_limit_bytes=62 << 20), name="weight_grads",
-        cost_estimate=pl.CostEstimate(flops=5_500_000_000, bytes_accessed=32_000_000, transcendentals=0),
-    )(*acts, *grads)
+        partial(weights_kernel, table, groups, stride),
+        out_shape=jax.ShapeDtypeStruct((2, 4, 2, 2, rows, 128), bf16),
+        in_specs=[pl.BlockSpec(memory_space=pl.ANY)], out_specs=pl.BlockSpec(memory_space=pl.ANY),
+        scratch_shapes=scratch,
+        compiler_params=pltpu.CompilerParams(collective_id=ident, has_side_effects=True, vmem_limit_bytes=62 << 20),
+        name="spread_weights",
+    )(parts)
+
+
+def return_kernel(table, groups, stride, *refs):
+    n = len(groups)
+    acts, grads, small_src, out, small_out = refs[:9], refs[9:18], refs[18], refs[19], refs[20]
+    rest = refs[21:]
+    sides, halves, bufs, units = (rest[i * n:(i + 1) * n] for i in range(4))
+    flat, turned, mid, line, sem = rest[4 * n:]
+    p = Place()
+    p.greet(["c", "y", "x"])
+    w = Wires(p, sem)
+    lists, finishes = [], []
+    for g, mats in enumerate(groups):
+        u0, un, r0, rn = group_span(table, mats)
+        side, half, buf, unit = sides[g], halves[g], bufs[g], units[g]
+        own_sem = w.new()
+
+        def own(d, side=side):
+            return side.at[(p.c,) + p.at(d)]
+
+        def other(d, half=half):
+            return half.at[p.at(d)]
+
+        def done(mats=mats, side=side, unit=unit, r0=r0, u0=u0, un=un, own_sem=own_sem):
+            mine = side.at[p.c, p.x, p.z, p.y]
+
+            def take(m, i):
+                lo = table[m][4] - r0 + i * table[m][5]
+                return mine[lo:lo + table[m][5], :].astype(jnp.float32)
+            panels_to_units(table, mats, take, flat, unit)
+            pltpu.make_async_copy(unit, out.at[p.z, p.y, p.c, pl.ds(u0, un)], sem.at[own_sem]).start()
+
+        ev, share, top = reduce_events(p, w, "zyx", own, other, buf, done)
+
+        def begin(mats=mats, side=side, share=share, r0=r0):
+            for m in mats:
+                lo, padded = table[m][4] - r0, table[m][5]
+
+                def put(t, i, v, lo=lo, padded=padded):
+                    v = v.reshape(4, 2, 2, padded, 128)
+                    rows = pl.ds(pl.multiple_of(lo + i * padded, 16), padded)
+                    side[0, t, :, :, rows, :] = v[:, :, 0]
+                    side[1, t, :, :, rows, :] = v[:, :, 1]
+                grad_panels(table, m, acts[m], grads[m], turned, put)
+            share(lambda d: side.at[(1 - p.c,) + p.at(d)])
+
+        def at(d, core, u0=u0, un=un):
+            _, z, y = p.at(d)
+            return out.at[z, y, core, pl.ds(u0, un)]
+
+        ag, finish = gather_events(p, w, "zy", unit, at)
+        lists.append([(-1, begin)] + ev + [(top + 1 + lv, a) for lv, a in ag])
+
+        def end(finish=finish, unit=unit, u0=u0, un=un, own_sem=own_sem):
+            finish()
+            pltpu.make_async_copy(unit, out.at[p.z, p.y, p.c, pl.ds(u0, un)], sem.at[own_sem]).wait()
+
+        finishes.append(end)
+    run_events(lists, stride, total_steps(p, w, small_src, small_out, mid, line))
+    for f in finishes:
+        f()
+    w.drain()
+
+
+def total_steps(p, w, src, out, mid, line):
+    k = [w.new(2) for _ in range(9)]
+    now = src
+    for i, way in enumerate(("c", "x", "y")):
+        w.send(k[i], now, mid.at[i], way)
+        yield
+        w.land(k[i], mid.at[i])
+        nxt = mid.at[3 + i] if i < 2 else line.at[p.z]
+        nxt[...] = now[...] + mid[i]
+        now = nxt
+    for i in range(4):
+        lo, hi = jnp.maximum(p.z - i, 0), jnp.minimum(p.z + i, 3)
+        if i > 0:
+            w.land(k[2 + i], line.at[lo], p.z >= i)
+            w.land(k[5 + i], line.at[hi], p.z + i <= 3)
+        if i < 3:
+            w.send(k[3 + i], line.at[lo], line.at[lo], "z+", jnp.logical_and(p.z >= i, p.z < 3))
+            w.send(k[6 + i], line.at[hi], line.at[hi], "z-", jnp.logical_and(p.z + i <= 3, p.z > 0))
+            yield
+    out[...] = (line[0] + line[1]) + (line[2] + line[3])
+
+
+def return_grads(acts, grads, small, table, total_units, groups, stride, ident):
+    spans = [group_span(table, m) for m in groups]
+    bf16 = jnp.bfloat16
+    scratch = [pltpu.VMEM((2, 2, 4, 2, s[3], 128), bf16) for s in spans]
+    scratch += [pltpu.VMEM((2, 4, 2, s[3], 128), bf16) for s in spans]
+    scratch += [pltpu.VMEM((edge_slots("zyx"), s[3], 128), bf16) for s in spans]
+    scratch += [pltpu.VMEM((s[1], 512), bf16) for s in spans]
+    scratch += [pltpu.VMEM((4 * max(s[1] for s in spans), 128), jnp.float32), pltpu.VMEM((FFE, 256), bf16),
+                pltpu.VMEM((5,) + small.shape, small.dtype), pltpu.VMEM((4,) + small.shape, small.dtype),
+                pltpu.SemaphoreType.DMA((len(groups) * (1 + 4 * 14 + 4 * 28) + 18,))]
+    vmem = pl.BlockSpec(memory_space=pltpu.VMEM)
+    return pl.pallas_call(
+        partial(return_kernel, table, groups, stride),
+        out_shape=(jax.ShapeDtypeStruct((4, 2, 2, total_units, 512), bf16), jax.ShapeDtypeStruct(small.shape, small.dtype)),
+        in_specs=[vmem] * 19, out_specs=(pl.BlockSpec(memory_space=pl.ANY), vmem),
+        scratch_shapes=scratch,
+        compiler_params=pltpu.CompilerParams(collective_id=ident, has_side_effects=True, vmem_limit_bytes=63 << 20),
+        name="return_grads",
+    )(*acts, *grads, small)
 
 
 def swap(v):
@@ -1128,7 +1201,7 @@
                     norm_biases, norm_first, norm_second, cotangent):
     t = lax.axis_index("tensor")
     shapes = weight_shapes(2)
-    table, _, _ = layout(shapes, 16)
+    table, _, rows = layout(shapes, 16)
 
     def whole(v, axis):
         own = lax.dynamic_index_in_dim(v, t, axis, keepdims=False)
@@ -1149,13 +1222,11 @@
     place = unit_places(unit, table, 16)
     parts = jnp.zeros((16 * SHARD_UNITS, 512), jnp.bfloat16)
     parts = parts.at[jnp.where(used, place, 16 * SHARD_UNITS)].set(master.astype(jnp.bfloat16), mode="drop", unique_indices=True)
-    shard = reduce_scatter(parts.reshape(4, 2, 2, SHARD_UNITS, 512), PLAN_DP, False, 1)
-    full = gather(to_panels(shard, table), PLAN_ALL, True, 2)
+    full = spread_weights(parts.reshape(4, 2, 2, SHARD_UNITS, 512), table, rows, GROUPS, 2, 1)
     kept = chain(tokens, pos, tile, norm_gains, norm_biases, cot, full, table)
     decoded, dx0, norms = kept[:3]
-    grads = weight_grads(kept[3:12], kept[12:21], table, full.shape[-2])
-    summed, norm_total = reduce_scatter(grads.reshape(full.shape), PLAN_ALL, True, 3, norms)
-    spread_out = gather(from_panels(summed, table), PLAN_DP, False, 4).reshape(16 * SHARD_UNITS, 512)
+    spread_out, norm_total = return_grads(kept[3:12], kept[12:21], norms, table, SHARD_UNITS, GROUPS, 3, 2)
+    spread_out = spread_out.reshape(16 * SHARD_UNITS, 512)
     reduced = jnp.where(used[:, None], jnp.take(spread_out, jnp.clip(place, 0, 16 * SHARD_UNITS - 1), axis=0).astype(jnp.float32), 0.0)
     new_master, new_first, new_second = adamw(master, reduced, first_moment, second_moment, WEIGHT_DECAY, LEARN_RATE)
     norm_params = jnp.concatenate([norm_gains, norm_biases], axis=0)

time: 536 us -> 473 us (0.88); the launches traced: 533 us -> 464 us
  Pallas kernels: 462 us -> 407 us
  local copies, waits for them, and re-layouts: 32 us -> 19.8 us
    pallas_call x5 -> x2, Pallas kernels: 399 us -> 344 us  [the longest x1 178 us: return_grads(): pl.pallas_call(partial(return_kernel, table, groups, stride), out_shape=(...]
    slice x12 -> x0, local copies, waits for them, and re-layouts: 9.34 us -> none  [the longest x7 5.08 us: from_panels(): m = rows[at:at + panels * padded].reshape(panels, padded, PANEL)[:, :rb]]
  transfers between devices with their start and end apart: 5 -> 5, of which waited for: 0 -> 0; matrix products, arithmetic and copies ran while one was open for 10% -> 10% of each run, Pallas kernels for 52% -> 74%
where the time goes in v3:
time: 473 us; the launch traced here: 464 us
  Pallas kernels  407 us (86%)
  other arithmetic  30.5 us (6%)
  local copies, waits for them, and re-layouts  19.8 us (4%)
  starting transfers between devices  5.21 us (1%)
    pallas_call x1, Pallas kernels, return_grads(): pl.pallas_call(partial(return_kernel, table, groups, stride), out_shape=(...  178 us
    pallas_call x1, Pallas kernels, spread_weights(): pl.pallas_call(partial(weights_kernel, table, groups, stride), out_shape=...  166 us
    pallas_call x1, Pallas kernels, chain(): pl.pallas_call(partial(chain_kernel, table), out_shape=outs, in_specs=[sp...  62.7 us
    scatter x1, other arithmetic, sequence_device(): parts.at[jnp.where(used, place, 16 * SHARD_UNITS)]  14.8 us
    gather x1, local copies, waits for them, and re-layouts, sequence_device(): jnp.take(spread_out, jnp.clip(place, 0, 16 * SHARD_UNITS - 1), axis=0)  11 us
  transfers between devices with their start and end apart: 5, of which 0 were waited for; matrix products, arithmetic and copies ran while one was open for 10% of the time, Pallas kernels for 74%

profile of v3, /device:TPU:1, one launch (start us, length us, event | category | flops | bytes accessed | tf_op | source)
XLA Modules:
  0.0 464.2 jit_solution(12501217101674075296)
XLA Ops:
  0.6 0.8 constant_dynamic-slice_fusion.4
  1.4 2.1 collective-permute-start.1
  3.5 0.9 dynamic-slice_bitcast_fusion.1
  4.4 0.1 collective-permute-start
  4.5 1.0 dynamic-slice_bitcast_fusion
  5.5 1.5 collective-permute-start.2
  7.0 0.9 compare_reduce_fusion
  7.9 0.1 fusion.7
  8.1 0.2 fusion.8
  8.2 0.1 select_reduce_fusion.1
  8.4 0.6 slice.7
  9.0 0.1 convert_reduce_fusion
  9.1 0.2 select_reduce_fusion
  9.3 0.7 fusion.5
  9.9 0.8 compare_and_fusion
  10.7 1.0 fusion.75
  11.8 1.2 fusion.76
  13.0 0.8 copy.31.tile_c
  13.8 14.8 %scatter_custom_fusion = bf16[10496,512]{1,0:T(8,128)(2,1)} fusion(s32[1296]{0:T(1024)S(1)} %get-tuple-element.55, bf16[]{:T(256)} %constant.216.clone.1, f32[1296,512]{1,0:T(8,128)} %param.17), kind=kCustom, calls=%fused_computation.2 | custom fusion | flops 663552 | bytes 13402114 | tf_op jit(solution)/shard_map/scatter | solution.py:1224
  28.6 0.0 copy-start.4
  28.6 0.0 copy-start.2
  28.6 165.7 %spread_weights.1 = bf16[2,4,2,2,2640,128]{5,4,3,2,1,0:T(8,128)(2,1)} custom-call(bf16[4,2,2,656,512]{4,3,2,1,0:T(8,128)(2,1)} %bitcast.37), custom_call_target="tpu_custom_call" | custom-call | tf_op jit(solution)/shard_map/spread_weights/pallas_call | solution.py:1081
  194.4 0.0 collective-permute-done.1
  194.4 0.8 copy.30
  195.2 0.0 collective-permute-done
  195.2 0.0 copy-done.4
  195.2 0.8 pad_maximum_fusion.3.tok
  196.0 0.0 collective-permute-done.2
  196.0 0.0 copy-done.2
  196.0 0.1 bitcast_select_fusion.1
  196.1 0.8 pad_maximum_fusion.1.cot
  196.9 62.7 %chain.1 = (f32[256,512]{1,0:T(8,128)}, f32[256,768]{1,0:T(8,128)}, f32[4,1280]{1,0:T(4,128)}, bf16[256,768]{1,0:T(8,128)(2,1)}, bf16[256,768]{1,0:T(8,128)(2,1)...) custom-call(bf16[256,768]{1,0:T(8,128)(2,1)} %pad_maximum_fusion.3.t, ...), custom_call_target="tpu_custom_call" | custom-call | flops 11000000512 | bytes 40000000 | tf_op jit(solution)/shard_map/chain/pallas_call | solution.py:817
  259.6 1.7 constant_dynamic-slice_fusion.1
  261.3 0.9 collective-permute-start.3
  262.1 1.0 constant_dynamic-slice_fusion
  263.2 0.7 collective-permute-start.4
  263.8 178.2 %return_grads.1 = (bf16[4,2,2,656,512]{4,3,2,1,0:T(8,128)(2,1)}, f32[4,1280]{1,0:T(4,128)}) custom-call(bf16[256,768]{1,0:T(8,128)(2,1)} %get-tuple-element.33.refs_0_, bf16[256,768]{1,0:T(8,128)(2,1)} %get-tuple-element.34.refs_1_, bf16[256,768]{1,0:T(8,128)(2,1)} %get-tuple-element.35.refs_2_, bf16[256,3072]{1,0:T(8,128)(2,1)} %get-tuple-element.36.refs_3_, ...), custom_call_target="tpu_custom_call" | custom-call | tf_op jit(solution)/shard_map/return_grads/pallas_call | solution.py:1186
  442.0 0.0 copy-start
  442.0 11.0 %gather_fusion = bf16[1296,512]{1,0:T(8,128)(2,1)} fusion(bf16[10496,512]{1,0:T(8,128)(2,1)} %bitcast.39, s32[2048]{0:T(1024)S(1)} %pad_clamp_fusion), kind=kCustom, calls=%fused_computation | custom fusion | bytes 2659392 | tf_op jit(solution)/shard_map/jit(_take)/gather | solution.py:1230
  453.0 0.0 copy-done
  453.0 0.0 copy-start.5
  453.0 0.0 copy-start.6
  453.0 0.0 copy-start.7
  453.0 0.0 copy-start.8
  453.0 0.0 copy-start.9
  453.1 0.0 copy-start.3
  453.1 0.0 copy-start.1
  453.1 7.2 %multiply_subtract_fusion = (f32[1296,512]{1,0:T(8,128)}, f32[1296,512]{1,0:T(8,128)}, f32[1296,512]{1,0:T(8,128)}) fusion(f32[1296,512]{1,0:T(8,128)S(1)} %copy-done, bf16[1296,512]{1,0:T(8,128)(2,1)} %gather_fusion, pred[1296]{0:T(1024)(128)(4,1)S(1)} %get-tuple-element.62, pred[1296]{0:T(1024)(128)(4,1)S(1)} %get-tuple-element.105, f32[1296,512]{1,0:T(8,128)} %param.18, ...), kind=kLoop, calls=%fused_computation.7 | loop fusion | flops 11280384 | bytes 17254944 | tf_op jit(solution)/shard_map/sub | solution.py:92
  460.3 0.0 copy-done.5
  460.3 0.0 copy-done.6
  460.3 0.0 copy-done.7
  460.3 0.0 copy-done.8
  460.3 0.0 copy-done.9
  460.3 0.7 multiply_subtract_fusion.1
  461.0 0.0 collective-permute-done.3
  461.0 0.0 copy-done.3
  461.0 1.0 select_bitcast_fusion.3
  462.0 0.8 pad_maximum_fusion.2
  462.8 0.0 collective-permute-done.4
  462.8 0.0 copy-done.1
  462.8 0.1 select_bitcast_fusion.1
  462.9 0.9 pad_maximum_fusion
  (8 shorter events, 0.1 us)
Async XLA Ops:
  1.4 192.9 %collective-permute-start.1 = (s32[3,128]{1,0:T(4,128)S(1)}, s32[3,128]{1,0:T(4,128)S(1)}, u32[]{:S(2)}, u32[]{:S(2)}) collective-permute-start(s32[3,128]{1,0:T(4,128)S(1)} %bitcast.41), channel_id=1, source_target_pairs={{0,1},{1,0},{2,3},{3,2},{4,5},{5,4},{6,7},{7,6},{8,9},{9,8},{10,11... | collective-permute-start | bytes 4616 | tf_op jit(solution)/shard_map/ppermute | solution.py:1197
  4.4 190.7 %collective-permute-start = (bf16[128,768]{1,0:T(8,128)(2,1)S(1)}, bf16[128,768]{1,0:T(8,128)(2,1)S(1)}, u32[]{:S(2)}, u32[]{:S(2)}) collective-permute-start(bf16[128,768]{1,0:T(8,128)(2,1)S(1)} %dynamic-slice_bitcast_fusion.1), channel_id=1, source_target_pairs={{0,1},{1,0},{2,3},{3,2},{4,5},{5,4},{6,7},{7,6},{8,9},{9,8},{10,11... | collective-permute-start | bytes 589832 | tf_op jit(solution)/shard_map/ppermute | solution.py:1197
  5.5 190.5 %collective-permute-start.2 = (f32[128,512]{1,0:T(8,128)S(1)}, f32[128,512]{1,0:T(8,128)S(1)}, u32[]{:S(2)}, u32[]{:S(2)}) collective-permute-start(f32[128,512]{1,0:T(8,128)S(1)} %dynamic-slice_bitcast_fusion), channel_id=1, source_target_pairs={{0,1},{1,0},{2,3},{3,2},{4,5},{5,4},{6,7},{7,6},{8,9},{9,8},{10,11... | collective-permute-start | bytes 786440 | tf_op jit(solution)/shard_map/ppermute | solution.py:1197
  28.6 166.5 %copy-start.4 = (bf16[2,128,768]{2,1,0:T(8,128)(2,1)S(1)}, bf16[2,128,768]{2,1,0:T(8,128)(2,1)}, u32[]{:S(2)}) copy-start(bf16[2,128,768]{2,1,0:T(8,128)(2,1)} %param.13) | copy-start | bytes 1179652
  28.6 167.4 %copy-start.2 = (f32[2,128,512]{2,1,0:T(8,128)S(1)}, f32[2,128,512]{2,1,0:T(8,128)}, u32[]{:S(2)}) copy-start(f32[2,128,512]{2,1,0:T(8,128)} %param.24) | copy-start | bytes 1572868
  261.3 199.7 %collective-permute-start.3 = (f32[128,512]{1,0:T(8,128)}, f32[128,512]{1,0:T(8,128)}, u32[]{:S(2)}, u32[]{:S(2)}) collective-permute-start(f32[128,512]{1,0:T(8,128)} %constant_dynamic-slice_fusion.1), channel_id=1, source_target_pairs={{0,1},{1,0},{2,3},{3,2},{4,5},{5,4},{6,7},{7,6},{8,9},{9,8},{10,11... | collective-permute-start | bytes 786440 | tf_op jit(solution)/shard_map/ppermute | solution.py:1197
  263.2 199.6 %collective-permute-start.4 = (f32[128,768]{1,0:T(8,128)S(1)}, f32[128,768]{1,0:T(8,128)S(1)}, u32[]{:S(2)}, u32[]{:S(2)}) collective-permute-start(f32[128,768]{1,0:T(8,128)S(1)} %constant_dynamic-slice_fusion), channel_id=1, source_target_pairs={{0,1},{1,0},{2,3},{3,2},{4,5},{5,4},{6,7},{7,6},{8,9},{9,8},{10,11... | collective-permute-start | bytes 1179656 | tf_op jit(solution)/shard_map/ppermute | solution.py:1197
  442.0 11.0 %copy-start = (f32[1296,512]{1,0:T(8,128)S(1)}, f32[1296,512]{1,0:T(8,128)}, u32[]{:S(2)}) copy-start(f32[1296,512]{1,0:T(8,128)} %param.17) | copy-start | bytes 7962628
  453.0 7.2 %copy-start.5 = (f32[4,1280]{1,0:T(4,128)S(1)}, f32[4,1280]{1,0:T(4,128)}, u32[]{:S(2)}) copy-start(f32[4,1280]{1,0:T(4,128)} %param.22) | copy-start | bytes 61444
  453.0 7.2 %copy-start.6 = (f32[4,1280]{1,0:T(4,128)S(1)}, f32[4,1280]{1,0:T(4,128)}, u32[]{:S(2)}) copy-start(f32[4,1280]{1,0:T(4,128)} %param.23) | copy-start | bytes 61444
  453.0 7.2 %copy-start.7 = (f32[4,1280]{1,0:T(4,128)S(1)}, f32[4,1280]{1,0:T(4,128)}, u32[]{:S(2)}) copy-start(f32[4,1280]{1,0:T(4,128)} %get-tuple-element.53) | copy-start | bytes 61444
  453.0 7.2 %copy-start.8 = (f32[2,1280]{1,0:T(2,128)S(1)}, f32[2,1280]{1,0:T(2,128)}, u32[]{:S(2)}) copy-start(f32[2,1280]{1,0:T(2,128)} %gains.1) | copy-start | bytes 30724
  453.0 7.2 %copy-start.9 = (f32[2,1280]{1,0:T(2,128)S(1)}, f32[2,1280]{1,0:T(2,128)}, u32[]{:S(2)}) copy-start(f32[2,1280]{1,0:T(2,128)} %biases.1) | copy-start | bytes 30724
  453.1 7.9 %copy-start.3 = (f32[256,512]{1,0:T(8,128)S(1)}, f32[256,512]{1,0:T(8,128)}, u32[]{:S(2)}) copy-start(f32[256,512]{1,0:T(8,128)} %get-tuple-element.31) | copy-start | bytes 1572868
  453.1 9.7 %copy-start.1 = (f32[256,768]{1,0:T(8,128)S(1)}, f32[256,768]{1,0:T(8,128)}, u32[]{:S(2)}) copy-start(f32[256,768]{1,0:T(8,128)} %get-tuple-element.32) | copy-start | bytes 2359300
